TPU v7x, 512 devices: a whole 4x8x8 slice. The times are simulated.
512 devices in a mesh: expert: 32 (over x, y), dp: 16 (over z, core).
Axes of the slice: x: 4, y: 8, z: 8, core: 2. Of those that a mesh axis runs over, the one named last changes fastest.
Arguments:
- frames_in: bfloat16 [32, 2048, 1536], P('expert', 'dp'), may hold values from -6 to 6
- conv_kernel: bfloat16 [31, 1536], replicated, may hold values from -1 to 1
- norm_gain: bfloat16 [1536], replicated, may hold values from 0.099609375 to 1.8984375
- router: bfloat16 [1536, 32], replicated, may hold values from -0.15625 to 0.15625
- w_in: bfloat16 [32, 3072, 1536], P('expert', 'dp'), may hold values from -0.15625 to 0.15625
- w_out: bfloat16 [32, 3072, 1536], P('expert', 'dp'), may hold values from -0.109375 to 0.109375
- routes: int32 [32, 2048, 2], P('expert', 'dp'), may hold values from 0 to 31, all different within a row; in each aligned block of 128 rows (0 to 127, 128 to 255, ..., all dimensions but the last counted through in order) at most 9 rows name the same one
Outputs:
- block_output: bfloat16 [32, 2048, 1536], P('expert', 'dp')
Inputs may be any that keep to these rules, and one draw needn't show every extreme that they name: `routes`: each frame names 2 different experts. In each aligned block of 128 frames of an utterance (the frames of one device) no expert is named more than 9 times, a bound that some block reaches.
All inputs are finite; a program needn't handle non-finite values.
Results may differ from a plain program's by a relative error of at most 0.007.
Values may be sent and summed in bfloat16 or wider, within the bound.
No kernel may reach another device: no remote copies, remote signals or barrier semaphores. Data moves between devices by JAX's collectives and lax.ppermute only.
A program may use at most 64 MiB of HBM per device.

v0:
```python
import jax
import jax.numpy as jnp
from jax import lax
from jax.sharding import PartitionSpec as P


def swapped(value, axis, distance):
    mask = 2**distance
    pairs = [(source, source ^ mask) for source in range(lax.axis_size(axis))]
    return lax.ppermute(value, axis, pairs)


def extended(block, sides, width):
    for axis, dim in sides:
        count = lax.axis_size(axis)
        forward = [(i, i + 1) for i in range(count - 1)]
        backward = [(target, source) for source, target in forward]
        low = lax.ppermute(
            lax.slice_in_dim(block, block.shape[dim] - width, None, axis=dim), axis, forward
        )
        high = lax.ppermute(lax.slice_in_dim(block, 0, width, axis=dim), axis, backward)
        block = jnp.concatenate([low, block, high], axis=dim)
    return block


def expert_block(rows, first_w, second_w, row_bits, bit_count):
    place = lax.axis_index("dp")
    for bit in range(row_bits):
        other = swapped(rows, "dp", bit)
        upper = place >> bit & 1 == 1
        rows = jnp.concatenate(
            [jnp.where(upper, other, rows), jnp.where(upper, rows, other)], axis=0
        )
    stacked = jnp.stack([first_w, second_w])
    for bit in range(row_bits, bit_count):
        other = swapped(stacked, "dp", bit)
        stacked = jnp.concatenate([stacked, other], axis=1)
    preact = lax.dot_general(
        rows, stacked[0], (((1,), (1,)), ((), ())), preferred_element_type=jnp.float32
    )
    hidden = jax.nn.silu(preact).astype(jnp.bfloat16)
    partial_value = jnp.dot(hidden, stacked[1], preferred_element_type=jnp.float32)
    for bit in reversed(range(row_bits)):
        half_rows = partial_value.shape[0] // 2
        first_half = partial_value[:half_rows]
        second_half = partial_value[half_rows:]
        upper = place >> bit & 1 == 1
        outgoing = jnp.where(upper, first_half, second_half)
        kept = jnp.where(upper, second_half, first_half)
        partial_value = kept + swapped(outgoing.astype(jnp.bfloat16), "dp", bit).astype(
            outgoing.dtype
        )
    return partial_value


def shards(frames_in, conv_kernel, norm_gain, router, w_in, w_out, routes):
    tok_rows = frames_in.shape[1]
    features = frames_in.shape[2]
    kernel_len = conv_kernel.shape[0]
    margin = (kernel_len - 1) // 2
    padded = extended(frames_in, (("dp", 1),), margin)
    frames_f = frames_in[0].astype(jnp.float32)
    convolved = jnp.zeros((tok_rows, features), jnp.float32)
    for offset in range(kernel_len):
        convolved = convolved + conv_kernel[offset].astype(jnp.float32) * padded[
            0, offset : offset + tok_rows
        ].astype(jnp.float32)
    residual = frames_f + jax.nn.silu(convolved)
    scale_rms = lax.rsqrt(jnp.mean(residual * residual, axis=-1, keepdims=True) + 1e-06)
    normed = (residual * scale_rms * norm_gain.astype(jnp.float32)).astype(jnp.bfloat16)
    logits = jnp.dot(normed, router, preferred_element_type=jnp.float32)
    expert_count = router.shape[1]
    chosen = routes[0]
    top_k = chosen.shape[1]
    onehot = (chosen[:, :, None] == jnp.arange(expert_count, dtype=jnp.int32)).astype(jnp.float32)
    gating = jax.nn.sigmoid(jnp.sum(onehot * logits[:, None, :], axis=-1))
    pair_count = tok_rows * top_k
    flat_hot = onehot.reshape(pair_count, expert_count)
    positions = jnp.arange(pair_count, dtype=jnp.int32)
    earlier = (positions[:, None] > positions[None, :]).astype(jnp.float32)
    counts = jnp.dot(earlier, flat_hot, precision=lax.Precision.HIGHEST)
    slot_of = jnp.sum(counts * flat_hot, axis=-1).astype(jnp.int32)
    capacity = max(2, 9 * top_k * tok_rows // (8 * lax.axis_size("expert")))
    target = chosen.reshape(pair_count) * capacity + slot_of
    placing = (
        jnp.arange(expert_count * capacity, dtype=jnp.int32)[:, None] == target[None, :]
    ).astype(jnp.bfloat16)
    normed_rep = jnp.repeat(normed, top_k, axis=0)
    sent_normed = (
        jnp.dot(placing, normed_rep, preferred_element_type=jnp.float32)
        .astype(jnp.bfloat16)
        .reshape(expert_count, capacity, features)
    )
    received = lax.all_to_all(sent_normed, "expert", split_axis=0, concat_axis=0, tiled=True)
    slot_block = received.reshape(expert_count * capacity, features)
    bit_count = lax.axis_size("dp").bit_length() - 1
    row_bits = bit_count // 2
    summed = expert_block(slot_block, w_in[0], w_out[0], row_bits, bit_count)
    expert_out = summed.astype(jnp.bfloat16).reshape(expert_count, capacity, features)
    returned = lax.all_to_all(
        expert_out, "expert", split_axis=0, concat_axis=0, tiled=True
    ).reshape(expert_count * capacity, features)
    pulled_back = lax.dot_general(
        placing, returned, (((0,), (0,)), ((), ())), preferred_element_type=jnp.float32
    )
    pulled_back = pulled_back.reshape(tok_rows, top_k, features)
    combined = (residual + jnp.sum(gating[:, :, None] * pulled_back, axis=1)).astype(jnp.bfloat16)
    return combined[None]


def solution(mesh):
    return jax.shard_map(
        shards,
        mesh=mesh,
        in_specs=(
            P("expert", "dp", None),
            P(),
            P(),
            P(),
            P("expert", "dp", None),
            P("expert", "dp", None),
            P("expert", "dp", None),
        ),
        out_specs=P("expert", "dp", None),
        check_vma=False,
    )
```

profile of v0, /device:TPU:8, one launch (start us, length us, event | category | flops | bytes accessed | tf_op | source)
XLA Modules:
  0.0 373.2 jit_solution(8222266608243639774)
XLA Ops:
  0.9 1.7 collective-permute-start
  2.6 1.3 collective-permute-start.1
  6.1 1.6 convert_reduce_fusion.30
  7.9 1.3 convert_reduce_fusion.29
  10.0 9.2 %multiply_reduce_fusion = (f32[128]{0:T(128)S(1)}, f32[128,1536]{1,0:T(8,128)S(1)}) fusion(bf16[1,143,1536]{2,1,0:T(8,128)(2,1)S(1)} %constant_dynamic-update-slice_fusion, f32[1536]{0:T(1024)S(1)} %get-tuple-element.34, f32[1536]{0:T(1024)S(1)} %get-tuple-element.35, f32[1536]{0:T(1024)S(1)} %get-tuple-element.6, f32[1536]{0:T(1024)S(1)} %get-tuple-element.7, ...), kind=kLoop, calls=%fused_computation.197 | loop fusion | flops 28311424 | bytes 7314944 | tf_op jit(solution)/shard_map/reduce_sum | solution.py:69
  21.6 1.4 reshape.353
  22.9 10.2 %all-to-all-start = ((bf16[32,9,1536]{2,1,0:T(8,128)(2,1)}), bf16[32,9,1536]{2,1,0:T(8,128)(2,1)S(1)}, u32[]{:S(2)}, u32[]{:S(2)}) async-start(bf16[32,9,1536]{2,1,0:T(8,128)(2,1)} %reshape.353), calls=%async_computation | async-start | bytes 3145728 | tf_op jit(solution)/shard_map/all_to_all | solution.py:94
  35.3 8.6 %collective-permute-start.4 = (bf16[2,192,1536]{2,1,0:T(8,128)(2,1)S(1)}, bf16[2,192,1536]{2,1,0:T(8,128)(2,1)}, u32[]{:S(2)}, u32[]{:S(2)}) collective-permute-start(bf16[2,192,1536]{2,1,0:T(8,128)(2,1)S(1)} %constant_dynamic-update-slice_fusion.2), channel_id=1, source_target_pairs={{0,4},{1,5},{2,6},{3,7},{4,0},{5,1},{6,2},{7,3},{8,12},{9,13},{10,... | collective-permute-start | bytes 3538952 | tf_op jit(solution)/shard_map/ppermute | solution.py:10
  43.9 27.5 %all-to-all-done = bf16[32,9,1536]{2,1,0:T(8,128)(2,1)S(1)} async-done(((bf16[32,9,1536]{2,1,0:T(8,128)(2,1)}), bf16[32,9,1536]{2,1,0:T(8,128)(2,1)S(1)}, u32[]{:S(2)}, u32[]{:S(2)}) %all-to-all-start) | async-done | bytes 884768 | tf_op jit(solution)/shard_map/all_to_all | solution.py:94
  72.6 4.2 %collective-permute-start.2 = (bf16[288,1536]{1,0:T(8,128)(2,1)}, bf16[288,1536]{1,0:T(8,128)(2,1)}, u32[]{:S(2)}, u32[]{:S(2)}) collective-permute-start(bf16[288,1536]{1,0:T(8,128)(2,1)} %reshape.354), channel_id=1, source_target_pairs={{0,1},{1,0},{2,3},{3,2},{4,5},{5,4},{6,7},{7,6},{8,9},{9,8},{10,11... | collective-permute-start | bytes 2654216 | tf_op jit(solution)/shard_map/ppermute | solution.py:10
  76.8 18.8 %collective-permute-done.4 = bf16[2,192,1536]{2,1,0:T(8,128)(2,1)} collective-permute-done((bf16[2,192,1536]{2,1,0:T(8,128)(2,1)S(1)}, bf16[2,192,1536]{2,1,0:T(8,128)(2,1)}, u32[]{:S(2)}, u32[]{:S(2)}) %collective-permute-start.4) | collective-permute-done | bytes 1179680 | tf_op jit(solution)/shard_map/ppermute | solution.py:10
  95.6 2.8 pad_maximum_fusion.1
  98.5 8.5 %collective-permute-start.5 = (bf16[2,384,1536]{2,1,0:T(8,128)(2,1)}, bf16[2,384,1536]{2,1,0:T(8,128)(2,1)}, u32[]{:S(2)}, u32[]{:S(2)}) collective-permute-start(bf16[2,384,1536]{2,1,0:T(8,128)(2,1)} %pad_maximum_fusion.1), channel_id=1, source_target_pairs={{0,8},{1,9},{2,10},{3,11},{4,12},{5,13},{6,14},{7,15},{8,0},{9,1},... | collective-permute-start | bytes 7077896 | tf_op jit(solution)/shard_map/ppermute | solution.py:10
  106.9 1.6 broadcast_select_fusion.3
  108.5 1.4 pad_maximum_fusion.2
  109.9 2.1 collective-permute-start.3
  112.0 97.6 %collective-permute-done.5 = bf16[2,384,1536]{2,1,0:T(8,128)(2,1)} collective-permute-done((bf16[2,384,1536]{2,1,0:T(8,128)(2,1)}, bf16[2,384,1536]{2,1,0:T(8,128)(2,1)}, u32[]{:S(2)}, u32[]{:S(2)}) %collective-permute-start.5) | collective-permute-done | bytes 2359328 | tf_op jit(solution)/shard_map/ppermute | solution.py:10
  209.7 3.8 %pad_maximum_fusion = bf16[2,768,1536]{2,1,0:T(8,128)(2,1)} fusion(bf16[2,384,1536]{2,1,0:T(8,128)(2,1)} %collective-permute-done.5, bf16[2,192,1536]{2,1,0:T(8,128)(2,1)} %collective-permute-done.4, bf16[2,192,1536]{2,1,0:T(8,128)(2,1)S(1)} %constant_dynamic-update-slice_fusion.2), kind=kLoop, calls=%fused_computation | loop fusion | flops 14155776 | bytes 9437184 | tf_op jit(solution)/shard_map/concatenate | solution.py:37
  213.4 31.8 %collective-permute-done.3 = bf16[576,1536]{1,0:T(8,128)(2,1)} collective-permute-done((bf16[576,1536]{1,0:T(8,128)(2,1)}, bf16[576,1536]{1,0:T(8,128)(2,1)}, u32[]{:S(2)}, u32[]{:S(2)}) %collective-permute-start.3) | collective-permute-done | bytes 1769504 | tf_op jit(solution)/shard_map/ppermute | solution.py:10
  245.3 4.0 %broadcast_select_fusion.1 = (bf16[576,1536]{1,0:T(8,128)(2,1)}, bf16[576,1536]{1,0:T(8,128)(2,1)}) fusion(bf16[576,1536]{1,0:T(8,128)(2,1)} %collective-permute-done.3, pred[]{:T(512)S(6)} %eq.71, bf16[288,1536]{1,0:T(8,128)(2,1)S(1)} %get-tuple-element.41, bf16[288,1536]{1,0:T(8,128)(2,1)S(1)} %get-tuple-element.40), kind=kLoop, calls=%fused_computation.33 | loop fusion | flops 5308416 | bytes 7077889 | tf_op jit(solution)/shard_map/jit(_where)/select_n | solution.py:32
  249.2 13.2 %fusion.6 = f32[1152,1536]{1,0:T(8,128)} fusion(bf16[2,768,1536]{2,1,0:T(8,128)(2,1)} %pad_maximum_fusion, bf16[576,1536]{1,0:T(8,128)(2,1)} %get-tuple-element.39, bf16[576,1536]{1,0:T(8,128)(2,1)} %get-tuple-element.38), kind=kOutput, calls=%fused_computation.11 | convolution fusion | flops 5447319552 | bytes 15335424 | tf_op jit(solution)/shard_map/dot_general | solution.py:42
  262.5 3.4 select_convert_fusion
  265.9 2.2 collective-permute-start.6
  268.1 38.1 %collective-permute-done.6 = bf16[576,1536]{1,0:T(8,128)(2,1)S(1)} collective-permute-done((bf16[576,1536]{1,0:T(8,128)(2,1)S(1)}, bf16[576,1536]{1,0:T(8,128)(2,1)S(1)}, u32[]{:S(2)}, u32[]{:S(2)}) %collective-permute-start.6) | collective-permute-done | bytes 1769504 | tf_op jit(solution)/shard_map/ppermute | solution.py:10
  306.2 4.0 %convert_add_fusion = f32[576,1536]{1,0:T(8,128)S(1)} fusion(bf16[576,1536]{1,0:T(8,128)(2,1)S(1)} %collective-permute-done.6, f32[1152,1536]{1,0:T(8,128)} %fusion.6, pred[]{:T(512)S(6)} %eq.71), kind=kLoop, calls=%fused_computation.5 | loop fusion | flops 2654208 | bytes 12386305 | tf_op jit(solution)/shard_map/add | solution.py:50
  310.4 1.9 collective-permute-start.7
  312.3 2.4 collective-permute-done.7
  315.1 1.4 reshape.355
  316.5 9.9 %all-to-all-start.1 = ((bf16[32,9,1536]{2,1,0:T(8,128)(2,1)}), bf16[32,9,1536]{2,1,0:T(8,128)(2,1)S(1)}, u32[]{:S(2)}, u32[]{:S(2)}) async-start(bf16[32,9,1536]{2,1,0:T(8,128)(2,1)} %reshape.355), calls=%async_computation.1 | async-start | bytes 3145728 | tf_op jit(solution)/shard_map/all_to_all | solution.py:100
  328.3 37.1 %all-to-all-done.1 = bf16[32,9,1536]{2,1,0:T(8,128)(2,1)S(1)} async-done(((bf16[32,9,1536]{2,1,0:T(8,128)(2,1)}), bf16[32,9,1536]{2,1,0:T(8,128)(2,1)S(1)}, u32[]{:S(2)}, u32[]{:S(2)}) %all-to-all-start.1) | async-done | bytes 884768 | tf_op jit(solution)/shard_map/all_to_all | solution.py:100
  365.8 1.6 fusion.10
  367.5 5.5 %fusion.105 = bf16[1,128,1536]{2,1,0:T(8,128)(2,1)} fusion(bf16[1,128,1536]{2,1,0:T(8,128)(2,1)S(1)} %copy-done.1, f32[128,1536]{1,0:T(8,128)S(1)} %fusion.10, bf16[1,15,1536]{2,1,0:T(8,128)(2,1)S(1)} %collective-permute-done, f32[1536]{0:T(1024)} %copy-done.43, f32[1536]{0:T(1024)} %copy-done.44, f32[1536]{0:T(1024)S(1)} %get-tuple-element.6, ...), kind=kLoop, calls=%fused_computation.195 | loop fusion | flops 28311552 | bytes 7707648 | tf_op jit(solution)/shard_map/convert_element_type | solution.py:107
  (123 shorter events, 12.0 us)
Async XLA Ops:
  0.0 327.4 %copy-start = (bf16[1536,32]{0,1:T(8,128)(2,1)S(1)}, bf16[1536,32]{0,1:T(8,128)(2,1)}, u32[]{:S(2)}) copy-start(bf16[1536,32]{0,1:T(8,128)(2,1)} %param.10) | copy-start | bytes 294916
  0.9 9.1 %collective-permute-start = (bf16[1,15,1536]{2,1,0:T(8,128)(2,1)S(1)}, bf16[1,15,1536]{2,1,0:T(8,128)(2,1)S(1)}, u32[]{:S(2)}, u32[]{:S(2)}) collective-permute-start(bf16[1,15,1536]{2,1,0:T(8,128)(2,1)S(1)} %get-tuple-element.42), channel_id=1, source_target_pairs={{0,1},{1,2},{2,3},{3,4},{4,5},{5,6},{6,7},{7,8},{8,9},{9,10},{10,1... | collective-permute-start | bytes 138248 | tf_op jit(solution)/shard_map/ppermute | solution.py:18
  2.6 7.4 %collective-permute-start.1 = (bf16[1,15,1536]{2,1,0:T(8,128)(2,1)S(1)}, bf16[1,15,1536]{2,1,0:T(8,128)(2,1)S(1)}, u32[]{:S(2)}, u32[]{:S(2)}) collective-permute-start(bf16[1,15,1536]{2,1,0:T(8,128)(2,1)S(1)} %get-tuple-element.43), channel_id=1, source_target_pairs={{1,0},{2,1},{3,2},{4,3},{5,4},{6,5},{7,6},{8,7},{9,8},{10,9},{11,1... | collective-permute-start | bytes 138248 | tf_op jit(solution)/shard_map/ppermute | solution.py:21
  6.1 15.1 %copy-start.45 = (s32[256]{0:T(256)}, s32[256]{0:T(256)S(1)}, u32[]{:S(2)}) copy-start(s32[256]{0:T(256)S(1)} %convert_add_fusion.2) | copy-start | bytes 3076
  7.7 11.5 %copy-start.4 = (f32[1536]{0:T(1024)}, f32[1536]{0:T(1024)S(1)}, u32[]{:S(2)}) copy-start(f32[1536]{0:T(1024)S(1)} %get-tuple-element.7) | copy-start | bytes 18436
  7.7 11.5 %copy-start.6 = (f32[1536]{0:T(1024)}, f32[1536]{0:T(1024)S(1)}, u32[]{:S(2)}) copy-start(f32[1536]{0:T(1024)S(1)} %get-tuple-element.8) | copy-start | bytes 18436
  7.7 11.5 %copy-start.8 = (f32[1536]{0:T(1024)}, f32[1536]{0:T(1024)S(1)}, u32[]{:S(2)}) copy-start(f32[1536]{0:T(1024)S(1)} %get-tuple-element.9) | copy-start | bytes 18436
  7.8 11.5 %copy-start.10 = (f32[1536]{0:T(1024)}, f32[1536]{0:T(1024)S(1)}, u32[]{:S(2)}) copy-start(f32[1536]{0:T(1024)S(1)} %get-tuple-element.10) | copy-start | bytes 18436
  7.8 11.5 %copy-start.12 = (f32[1536]{0:T(1024)}, f32[1536]{0:T(1024)S(1)}, u32[]{:S(2)}) copy-start(f32[1536]{0:T(1024)S(1)} %get-tuple-element.11) | copy-start | bytes 18436
  7.8 11.5 %copy-start.14 = (f32[1536]{0:T(1024)}, f32[1536]{0:T(1024)S(1)}, u32[]{:S(2)}) copy-start(f32[1536]{0:T(1024)S(1)} %get-tuple-element.12) | copy-start | bytes 18436
  7.8 11.5 %copy-start.16 = (f32[1536]{0:T(1024)}, f32[1536]{0:T(1024)S(1)}, u32[]{:S(2)}) copy-start(f32[1536]{0:T(1024)S(1)} %get-tuple-element.13) | copy-start | bytes 18436
  22.9 48.6 %all-to-all-start = ((bf16[32,9,1536]{2,1,0:T(8,128)(2,1)}), bf16[32,9,1536]{2,1,0:T(8,128)(2,1)S(1)}, u32[]{:S(2)}, u32[]{:S(2)}) async-start(bf16[32,9,1536]{2,1,0:T(8,128)(2,1)} %reshape.353), calls=%async_computation | async-start | bytes 3145728 | tf_op jit(solution)/shard_map/all_to_all | solution.py:94
  35.3 60.3 %collective-permute-start.4 = (bf16[2,192,1536]{2,1,0:T(8,128)(2,1)S(1)}, bf16[2,192,1536]{2,1,0:T(8,128)(2,1)}, u32[]{:S(2)}, u32[]{:S(2)}) collective-permute-start(bf16[2,192,1536]{2,1,0:T(8,128)(2,1)S(1)} %constant_dynamic-update-slice_fusion.2), channel_id=1, source_target_pairs={{0,4},{1,5},{2,6},{3,7},{4,0},{5,1},{6,2},{7,3},{8,12},{9,13},{10,... | collective-permute-start | bytes 3538952 | tf_op jit(solution)/shard_map/ppermute | solution.py:10
  72.6 34.3 %collective-permute-start.2 = (bf16[288,1536]{1,0:T(8,128)(2,1)}, bf16[288,1536]{1,0:T(8,128)(2,1)}, u32[]{:S(2)}, u32[]{:S(2)}) collective-permute-start(bf16[288,1536]{1,0:T(8,128)(2,1)} %reshape.354), channel_id=1, source_target_pairs={{0,1},{1,0},{2,3},{3,2},{4,5},{5,4},{6,7},{7,6},{8,9},{9,8},{10,11... | collective-permute-start | bytes 2654216 | tf_op jit(solution)/shard_map/ppermute | solution.py:10
  98.5 111.2 %collective-permute-start.5 = (bf16[2,384,1536]{2,1,0:T(8,128)(2,1)}, bf16[2,384,1536]{2,1,0:T(8,128)(2,1)}, u32[]{:S(2)}, u32[]{:S(2)}) collective-permute-start(bf16[2,384,1536]{2,1,0:T(8,128)(2,1)} %pad_maximum_fusion.1), channel_id=1, source_target_pairs={{0,8},{1,9},{2,10},{3,11},{4,12},{5,13},{6,14},{7,15},{8,0},{9,1},... | collective-permute-start | bytes 7077896 | tf_op jit(solution)/shard_map/ppermute | solution.py:10
  109.9 135.4 %collective-permute-start.3 = (bf16[576,1536]{1,0:T(8,128)(2,1)}, bf16[576,1536]{1,0:T(8,128)(2,1)}, u32[]{:S(2)}, u32[]{:S(2)}) collective-permute-start(bf16[576,1536]{1,0:T(8,128)(2,1)} %pad_maximum_fusion.2), channel_id=1, source_target_pairs={{0,2},{1,3},{2,0},{3,1},{4,6},{5,7},{6,4},{7,5},{8,10},{9,11},{10,... | collective-permute-start | bytes 5308424 | tf_op jit(solution)/shard_map/ppermute | solution.py:10
  265.9 40.4 %collective-permute-start.6 = (bf16[576,1536]{1,0:T(8,128)(2,1)S(1)}, bf16[576,1536]{1,0:T(8,128)(2,1)S(1)}, u32[]{:S(2)}, u32[]{:S(2)}) collective-permute-start(bf16[576,1536]{1,0:T(8,128)(2,1)S(1)} %select_convert_fusion), channel_id=1, source_target_pairs={{0,2},{1,3},{2,0},{3,1},{4,6},{5,7},{6,4},{7,5},{8,10},{9,11},{10,... | collective-permute-start | bytes 5308424 | tf_op jit(solution)/shard_map/ppermute | solution.py:10
  310.4 4.3 %collective-permute-start.7 = (bf16[288,1536]{1,0:T(8,128)(2,1)S(1)}, bf16[288,1536]{1,0:T(8,128)(2,1)S(1)}, u32[]{:S(2)}, u32[]{:S(2)}) collective-permute-start(bf16[288,1536]{1,0:T(8,128)(2,1)S(1)} %select_convert_fusion.1), channel_id=1, source_target_pairs={{0,1},{1,0},{2,3},{3,2},{4,5},{5,4},{6,7},{7,6},{8,9},{9,8},{10,11... | collective-permute-start | bytes 2654216 | tf_op jit(solution)/shard_map/ppermute | solution.py:10
  316.5 48.9 %all-to-all-start.1 = ((bf16[32,9,1536]{2,1,0:T(8,128)(2,1)}), bf16[32,9,1536]{2,1,0:T(8,128)(2,1)S(1)}, u32[]{:S(2)}, u32[]{:S(2)}) async-start(bf16[32,9,1536]{2,1,0:T(8,128)(2,1)} %reshape.355), calls=%async_computation.1 | async-start | bytes 3145728 | tf_op jit(solution)/shard_map/all_to_all | solution.py:100
  327.6 39.8 %copy-start.1 = (bf16[1,128,1536]{2,1,0:T(8,128)(2,1)S(1)}, bf16[1,128,1536]{2,1,0:T(8,128)(2,1)}, u32[]{:S(2)}) copy-start(bf16[1,128,1536]{2,1,0:T(8,128)(2,1)} %param.7) | copy-start | bytes 1179652
  327.6 39.9 %copy-start.5 = (f32[1536]{0:T(1024)S(1)}, f32[1536]{0:T(1024)}, u32[]{:S(2)}) copy-start(f32[1536]{0:T(1024)} %copy-done.4) | copy-start | bytes 18436
  327.6 39.8 %copy-start.7 = (f32[1536]{0:T(1024)S(1)}, f32[1536]{0:T(1024)}, u32[]{:S(2)}) copy-start(f32[1536]{0:T(1024)} %copy-done.6) | copy-start | bytes 18436
  327.6 39.8 %copy-start.9 = (f32[1536]{0:T(1024)S(1)}, f32[1536]{0:T(1024)}, u32[]{:S(2)}) copy-start(f32[1536]{0:T(1024)} %copy-done.8) | copy-start | bytes 18436
  327.6 39.8 %copy-start.11 = (f32[1536]{0:T(1024)S(1)}, f32[1536]{0:T(1024)}, u32[]{:S(2)}) copy-start(f32[1536]{0:T(1024)} %copy-done.10) | copy-start | bytes 18436
  327.6 39.8 %copy-start.13 = (f32[1536]{0:T(1024)S(1)}, f32[1536]{0:T(1024)}, u32[]{:S(2)}) copy-start(f32[1536]{0:T(1024)} %copy-done.12) | copy-start | bytes 18436
  327.6 39.8 %copy-start.15 = (f32[1536]{0:T(1024)S(1)}, f32[1536]{0:T(1024)}, u32[]{:S(2)}) copy-start(f32[1536]{0:T(1024)} %copy-done.14) | copy-start | bytes 18436
  327.7 39.8 %copy-start.17 = (f32[1536]{0:T(1024)S(1)}, f32[1536]{0:T(1024)}, u32[]{:S(2)}) copy-start(f32[1536]{0:T(1024)} %copy-done.16) | copy-start | bytes 18436
  327.7 39.8 %copy-start.19 = (f32[1536]{0:T(1024)S(1)}, f32[1536]{0:T(1024)}, u32[]{:S(2)}) copy-start(f32[1536]{0:T(1024)} %copy-done.18) | copy-start | bytes 18436
  327.7 39.8 %copy-start.21 = (f32[1536]{0:T(1024)S(1)}, f32[1536]{0:T(1024)}, u32[]{:S(2)}) copy-start(f32[1536]{0:T(1024)} %copy-done.20) | copy-start | bytes 18436
  327.7 39.8 %copy-start.23 = (f32[1536]{0:T(1024)S(1)}, f32[1536]{0:T(1024)}, u32[]{:S(2)}) copy-start(f32[1536]{0:T(1024)} %copy-done.22) | copy-start | bytes 18436
  327.7 39.8 %copy-start.25 = (f32[1536]{0:T(1024)S(1)}, f32[1536]{0:T(1024)}, u32[]{:S(2)}) copy-start(f32[1536]{0:T(1024)} %copy-done.24) | copy-start | bytes 18436
  327.7 39.8 %copy-start.27 = (f32[1536]{0:T(1024)S(1)}, f32[1536]{0:T(1024)}, u32[]{:S(2)}) copy-start(f32[1536]{0:T(1024)} %copy-done.26) | copy-start | bytes 18436
  (26 other events, 272.0 us)
where the time goes:
time: 374 us; the launch traced here: 373 us
  waiting for transfers between devices  253 us (68%)
  starting transfers between devices  50.6 us (14%)
  other arithmetic  40.6 us (11%)
  matrix products  15.6 us (4%)
  local copies, waits for them, and re-layouts  11.7 us (3%)
    ppermute x6, waiting for transfers between devices, swapped(): return lax.ppermute(value, axis, pairs)  189 us
    all_to_all x1, waiting for transfers between devices, shards(): lax.all_to_all(expert_out, 'expert', split_axis=0, concat_axis=0, tiled=T...  37.1 us
    all_to_all x1, waiting for transfers between devices, shards(): lax.all_to_all(sent_normed, 'expert', split_axis=0, concat_axis=0, tiled=...  27.5 us
    ppermute x6, starting transfers between devices, swapped(): return lax.ppermute(value, axis, pairs)  27.5 us
    dot_general x1, matrix products, expert_block(): jnp.dot(hidden, stacked[1], preferred_element_type=jnp.float32)  13.2 us
    all_to_all x1, starting transfers between devices, shards(): lax.all_to_all(sent_normed, 'expert', split_axis=0, concat_axis=0, tiled=...  10.2 us
    all_to_all x1, starting transfers between devices, shards(): lax.all_to_all(expert_out, 'expert', split_axis=0, concat_axis=0, tiled=T...  9.91 us
    reduce_sum x1, other arithmetic, shards(): jnp.mean(residual * residual, axis=-1, keepdims=True) + 1e-06  9.21 us
  transfers between devices with their start and end apart: 10, of which 7 were waited for; matrix products, arithmetic and copies ran while one was open for 5% of the time, Pallas kernels for 0%

commit v1 on v0

v1 whole, which is shorter than its diff:
```python
import functools

import jax
import jax.numpy as jnp
from jax import lax
from jax.experimental import pallas as pl
from jax.experimental.pallas import tpu as pltpu
from jax.sharding import PartitionSpec as P

MAIN = 8
LANES = 128
WIDE = 256
HALO = 16
bf16, f32, i32 = jnp.bfloat16, jnp.float32, jnp.int32
TRANSPOSED = (((1,), (1,)), ((), ()))


def dot(a, b):
    return jnp.dot(a, b, preferred_element_type=f32)


def iota(shape, dim):
    return lax.broadcasted_iota(i32, shape, dim)


def call(kernel, outs, args, flops, scratch=(), aliases={}, limit=48 << 20):
    moved = sum(x.size * x.dtype.itemsize for x in (*args, *outs))
    return pl.pallas_call(
        kernel,
        out_shape=outs,
        in_specs=[pl.BlockSpec(memory_space=pltpu.VMEM)] * len(args),
        out_specs=tuple(pl.BlockSpec(memory_space=pltpu.VMEM) for _ in outs),
        scratch_shapes=scratch,
        input_output_aliases=aliases,
        compiler_params=pltpu.CompilerParams(vmem_limit_bytes=limit),
        cost_estimate=pl.CostEstimate(flops=flops, bytes_accessed=moved, transcendentals=0),
    )(*args)


def shape(dims, dtype):
    return jax.ShapeDtypeStruct(dims, dtype)


def front_kernel(taps, x_ref, low_ref, high_ref, kernel_ref, gain_ref, router_ref, routes_ref,
                 sent_ref, res_ref, high_w_ref, low_w_ref, high_x_ref, low_x_ref, padded, kernels):
    tok, features = x_ref.shape
    tiles = features // LANES
    skip = HALO - (taps - 1) // 2
    for c in range(tiles):
        cols = slice(c * LANES, (c + 1) * LANES)
        padded[c, :HALO] = low_ref[:, cols].astype(f32)
        padded[c, HALO : HALO + tok] = x_ref[:, cols].astype(f32)
        padded[c, HALO + tok :] = high_ref[:, cols].astype(f32)
        kernels[c, :taps] = kernel_ref[:, cols].astype(f32)

    def column(c, squares):
        acc = jnp.zeros((tok, LANES), f32)
        for j in range(taps):
            acc = acc + kernels[c, pl.ds(j, 1), :] * padded[c, pl.ds(j + skip, tok), :]
        res = padded[c, pl.ds(HALO, tok), :] + acc / (1.0 + jnp.exp(-acc))
        res_ref[:, pl.ds(pl.multiple_of(c * LANES, LANES), LANES)] = res
        return squares + res * res

    squares = lax.fori_loop(0, tiles, column, jnp.zeros((tok, LANES), f32))
    mean = jnp.sum(squares, axis=-1, keepdims=True) / features
    scale = lax.rsqrt(mean + 1e-06)
    normed = (res_ref[...] * scale * gain_ref[...].astype(f32)).astype(bf16)

    experts = router_ref.shape[0]
    rows = experts * MAIN
    expert_of = iota((experts, tok), 0)
    hots = [(expert_of == routes_ref[k : k + 1, :]).astype(f32) for k in range(2)]
    before = (iota((tok, tok), 0) < iota((tok, tok), 1)).astype(bf16)
    counts = dot((hots[0] + hots[1]).astype(bf16), before)
    logits = lax.dot_general(router_ref[...], normed, TRANSPOSED, preferred_element_type=f32)
    place = iota((rows, tok), 0)
    main = jnp.zeros((rows, tok), f32)
    extra = jnp.zeros((rows, tok), f32)
    main_w = jnp.zeros((rows, tok), f32)
    extra_w = jnp.zeros((rows, tok), f32)
    for k in range(2):
        slot = jnp.sum(counts * hots[k], axis=0, keepdims=True).astype(i32)
        logit = jnp.sum(logits * hots[k], axis=0, keepdims=True)
        gate = 1.0 / (1.0 + jnp.exp(-logit))
        expert = routes_ref[k : k + 1, :]
        inside = slot < MAIN
        first = jnp.where(inside, expert * MAIN + slot, -1)
        hit = place == first
        main = main + hit.astype(f32)
        main_w = main_w + jnp.where(hit, gate, 0.0)
        last = jnp.where(inside, -1, expert)
        hit = lax.shift_right_arithmetic(place, 3) == last
        extra = extra + hit.astype(f32)
        extra_w = extra_w + jnp.where(hit, gate, 0.0)
    sent_ref[:, :features] = dot(main.astype(bf16), normed).astype(bf16)
    pieces = jnp.zeros((rows, WIDE), f32)
    piece_of = jnp.bitwise_and(place, MAIN - 1)
    for j in range(features // WIDE):
        chosen = jnp.where(piece_of == j, extra, 0.0).astype(bf16)
        pieces = pieces + dot(chosen, normed[:, j * WIDE : (j + 1) * WIDE])
    sent_ref[:, features:] = pieces.astype(bf16)
    for weights, high, low in ((main_w, high_w_ref, low_w_ref), (extra_w, high_x_ref, low_x_ref)):
        turned = weights.T
        coarse = turned.astype(bf16)
        high[...] = coarse
        low[...] = (turned - coarse.astype(f32)).astype(bf16)


def front(x, low, high, kernel, gain, router, routes):
    tok, features = x.shape
    taps = kernel.shape[0]
    rows = router.shape[0] * MAIN
    outs = (
        shape((rows, features + WIDE), bf16),
        shape((tok, features), f32),
        *(shape((tok, rows), bf16) for _ in range(4)),
    )
    tiles = features // LANES
    return call(
        functools.partial(front_kernel, taps),
        outs,
        (x, low, high, kernel, gain, router, routes),
        flops=20_000_000_000,
        scratch=[pltpu.VMEM((tiles, tok + 2 * HALO, LANES), f32), pltpu.VMEM((tiles, 32, LANES), f32)],
    )


def ffn(rows, blocks):
    first = jnp.concatenate([b[0] for b in blocks], axis=0)
    second = jnp.concatenate([b[1] for b in blocks], axis=0)
    preact = lax.dot_general(rows, first, TRANSPOSED, preferred_element_type=f32)
    hidden = (preact / (1.0 + jnp.exp(-preact))).astype(bf16)
    return hidden, second


def unpacked(packed_ref, rows_ref, base, features):
    count = packed_ref.shape[0]
    experts = count // MAIN
    rows_ref[base : base + count] = packed_ref[:, :features]
    pieces = packed_ref[:, features:]
    for j in range(features // WIDE):
        pick = (iota((experts, count), 1) == iota((experts, count), 0) * MAIN + j).astype(bf16)
        rows_ref[base + count : base + count + experts, j * WIDE : (j + 1) * WIDE] = dot(pick, pieces).astype(bf16)


def accumulate(hidden, second, out_ref, old_ref=None):
    for n in range(0, second.shape[1], 512):
        part = dot(hidden, second[:, n : n + 512])
        out_ref[:, n : n + 512] = part if old_ref is None else old_ref[:, n : n + 512] + part


def begin_kernel(mine_ref, other_ref, *refs):
    *blocks, rows_ref, total_ref = refs
    features = rows_ref.shape[1]
    unpacked(mine_ref, rows_ref, 0, features)
    unpacked(other_ref, rows_ref, rows_ref.shape[0] // 2, features)
    hidden, second = ffn(rows_ref[...], blocks)
    accumulate(hidden, second, total_ref)


def more_kernel(rows_ref, old_ref, *refs):
    *blocks, total_ref = refs
    hidden, second = ffn(rows_ref[...], blocks)
    accumulate(hidden, second, total_ref, old_ref)


def end_kernel(rows_ref, old_ref, *refs):
    *blocks, mine_ref, other_ref = refs
    hidden, second = ffn(rows_ref[...], blocks)
    half = rows_ref.shape[0] // 2
    for n in range(0, second.shape[1], 512):
        part = old_ref[:, n : n + 512] + dot(hidden, second[:, n : n + 512])
        mine_ref[:, n : n + 512] = part[:half]
        other_ref[:, n : n + 512] = part[half:].astype(bf16)


def pack_kernel(mine_ref, other_ref, packed_ref):
    count, features = packed_ref.shape[0], mine_ref.shape[1]
    experts = count // MAIN
    summed = (mine_ref[...] + other_ref[...].astype(f32)).astype(bf16)
    packed_ref[:, :features] = summed[:count]
    extra = summed[count:]
    pieces = jnp.zeros((count, WIDE), f32)
    for j in range(features // WIDE):
        place = (iota((count, experts), 0) == iota((count, experts), 1) * MAIN + j).astype(bf16)
        pieces = pieces + dot(place, extra[:, j * WIDE : (j + 1) * WIDE])
    packed_ref[:, features:] = pieces.astype(bf16)


def combine_kernel(back_ref, res_ref, high_w_ref, low_w_ref, high_x_ref, low_x_ref, out_ref):
    tok, features = res_ref.shape
    count = back_ref.shape[0]
    pieces = back_ref[:, features:]
    piece_of = jnp.bitwise_and(iota((tok, count), 1), MAIN - 1)
    for j in range(features // WIDE):
        cols = slice(j * WIDE, (j + 1) * WIDE)
        here = piece_of == j
        back = back_ref[:, cols]
        pulled = dot(high_w_ref[...], back) + dot(low_w_ref[...], back)
        for ref in (high_x_ref, low_x_ref):
            weights = jnp.where(here, ref[...].astype(f32), 0.0).astype(bf16)
            pulled = pulled + dot(weights, pieces)
        out_ref[:, cols] = (res_ref[:, cols] + pulled).astype(bf16)


def shards(frames_in, conv_kernel, norm_gain, router, w_in, w_out, routes):
    tok, features = frames_in.shape[1:]
    experts = router.shape[1]
    dp = lax.axis_size("dp")
    chips = dp // 2
    up = [(i, (i + 2) % dp) for i in range(dp)]
    down = [(i, (i - 2) % dp) for i in range(dp)]
    sibling = [(i, i ^ 1) for i in range(dp)]
    frames = frames_in[0]

    low = lax.ppermute(frames[tok - HALO :], "dp", [(i, i + 1) for i in range(dp - 1)])
    high = lax.ppermute(frames[:HALO], "dp", [(i + 1, i) for i in range(dp - 1)])

    own = jnp.concatenate([w_in, w_out], axis=0)
    a1, b1 = lax.ppermute(own, "dp", up), lax.ppermute(own, "dp", down)
    sent, residual, *weights = front(
        frames, low, high, conv_kernel, norm_gain[None], router.T, routes[0].T
    )
    sent, a1, b1 = lax.optimization_barrier((sent, a1, b1))
    a2, b2 = lax.ppermute(a1, "dp", up), lax.ppermute(b1, "dp", down)
    a3, b3 = lax.ppermute(a2, "dp", up), lax.ppermute(b2, "dp", down)
    half = own.shape[1] // 2
    a4, b4 = lax.ppermute(a3[:, :half], "dp", up), lax.ppermute(b3[:, half:], "dp", down)
    assert chips == 8

    def exchange(v):
        parts = v.reshape(experts, MAIN, v.shape[1])
        out = lax.all_to_all(parts, "expert", split_axis=0, concat_axis=0, tiled=True)
        return out.reshape(v.shape)

    mine = exchange(sent)
    other = lax.ppermute(mine, "dp", sibling)
    count = experts * (MAIN + 1)
    flops = lambda units: 2 * 2 * 2 * count * units * features
    units = own.shape[1]
    rows, total = call(
        begin_kernel,
        (shape((2 * count, features), bf16), shape((2 * count, features), f32)),
        (mine, other, own, a1, b1, a2, b2),
        flops(5 * units),
    )
    (total,) = call(
        more_kernel, (shape(total.shape, f32),), (rows, total, a3, b3), flops(2 * units), aliases={1: 0}
    )
    kept, gone = call(
        end_kernel,
        (shape((count, features), f32), shape((count, features), bf16)),
        (rows, total, a4, b4),
        flops(units),
    )
    came = lax.ppermute(gone, "dp", sibling)
    (packed,) = call(pack_kernel, (shape(sent.shape, bf16),), (kept, came), 10_000_000)
    back = exchange(packed)
    (out,) = call(combine_kernel, (shape((tok, features), bf16),), (back, residual, *weights), 10_000_000)
    return out[None]


def solution(mesh):
    rows = P("expert", "dp", None)
    return jax.shard_map(
        shards,
        mesh=mesh,
        in_specs=(rows, P(), P(), P(), rows, rows, rows),
        out_specs=rows,
        check_vma=False,
    )
```

time: 374 us -> 182 us (0.49)
  waiting for transfers between devices: 253 us -> 59.7 us
  other arithmetic: 40.6 us -> 0 us
  blocking collectives: 0 us -> 35.9 us
  Pallas kernels: 0 us -> 23.4 us
  matrix products: 15.6 us -> 0 us
  local copies, waits for them, and re-layouts: 11.7 us -> 6.89 us
  starting transfers between devices: 50.6 us -> 55.2 us
    ppermute x8 -> x12, waiting for transfers between devices: 189 us -> 59.7 us  [the longest x2 20.5 us: shards(): a2, b2 = (lax.ppermute(a1, 'dp', up), lax.ppermute(b1, 'dp', down))]
    all_to_all x2 -> x1, waiting for transfers between devices: 64.6 us -> 0.01 us  [exchange(): lax.all_to_all(parts, 'expert', split_axis=0, concat_axis=0, tiled=True)]
    all_to_all x0 -> x1, blocking collectives: none -> 35.9 us  [exchange(): lax.all_to_all(parts, 'expert', split_axis=0, concat_axis=0, tiled=True)]
    pallas_call x0 -> x6, Pallas kernels: none -> 23.4 us  [call(): pl.pallas_call(kernel, out_shape=outs, in_specs=[pl.BlockSpec(memory_spac...]
    dot_general x5 -> x0, matrix products: 15.6 us -> none  [the longest x1 13.2 us: expert_block(): jnp.dot(hidden, stacked[1], preferred_element_type=jnp.float32)]
    ppermute x8 -> x12, starting transfers between devices: 30.5 us -> 45.1 us  [the longest x2 15.4 us: shards(): a1, b1 = (lax.ppermute(own, 'dp', up), lax.ppermute(own, 'dp', down))]
    convert_element_type x6 -> x0, other arithmetic: 10.3 us -> none  [the longest x1 5.47 us: shards(): (residual + jnp.sum(gating[:, :, None] * pulled_back, axis=1)).astype(jnp...]
    all_to_all x2 -> x1, starting transfers between devices: 20.1 us -> 10.2 us  [exchange(): lax.all_to_all(parts, 'expert', split_axis=0, concat_axis=0, tiled=True)]
  transfers between devices with their start and end apart: 10 -> 13, of which waited for: 7 -> 7; matrix products, arithmetic and copies ran while one was open for 5% -> 1% of each run, Pallas kernels for 0% -> 10%
where the time goes in v1:
time: 182 us; the launch traced here: 181 us
  waiting for transfers between devices  59.7 us (33%)
  starting transfers between devices  55.2 us (30%)
  blocking collectives  35.9 us (20%)
  Pallas kernels  23.4 us (13%)
  local copies, waits for them, and re-layouts  6.89 us (4%)
    all_to_all x1, blocking collectives, exchange(): lax.all_to_all(parts, 'expert', split_axis=0, concat_axis=0, tiled=True)  35.9 us
    pallas_call x6, Pallas kernels, call(): pl.pallas_call(kernel, out_shape=outs, in_specs=[pl.BlockSpec(memory_spac...  23.4 us
    ppermute x2, waiting for transfers between devices, shards(): a2, b2 = (lax.ppermute(a1, 'dp', up), lax.ppermute(b1, 'dp', down))  20.5 us
    ppermute x2, waiting for transfers between devices, shards(): a1, b1 = (lax.ppermute(own, 'dp', up), lax.ppermute(own, 'dp', down))  19.1 us
    ppermute x2, waiting for transfers between devices, shards(): a3, b3 = (lax.ppermute(a2, 'dp', up), lax.ppermute(b2, 'dp', down))  17.7 us
    ppermute x2, starting transfers between devices, shards(): a1, b1 = (lax.ppermute(own, 'dp', up), lax.ppermute(own, 'dp', down))  15.4 us
    all_to_all x1, starting transfers between devices, exchange(): lax.all_to_all(parts, 'expert', split_axis=0, concat_axis=0, tiled=True)  10.2 us
    ppermute x2, starting transfers between devices, shards(): a3, b3 = (lax.ppermute(a2, 'dp', up), lax.ppermute(b2, 'dp', down))  7.6 us
  transfers between devices with their start and end apart: 13, of which 7 were waited for; matrix products, arithmetic and copies ran while one was open for 1% of the time, Pallas kernels for 10%

profile of v1, /device:TPU:8, one launch (start us, length us, event | category | flops | bytes accessed | tf_op | source)
XLA Modules:
  0.0 181.4 jit_solution(6546296747244824181)
XLA Ops:
  0.0 0.9 slice_bitcast_fusion
  0.9 1.7 collective-permute-start
  2.7 1.4 collective-permute-start.1
  4.1 1.1 constant_dynamic-update-slice_fusion.1
  5.3 6.8 %collective-permute-start.2 = (bf16[2,192,1536]{2,1,0:T(8,128)(2,1)S(1)}, bf16[2,192,1536]{2,1,0:T(8,128)(2,1)S(1)}, u32[]{:S(2)}, u32[]{:S(2)}) collective-permute-start(bf16[2,192,1536]{2,1,0:T(8,128)(2,1)S(1)} %constant_dynamic-update-slice_fusion.refs_0_), channel_id=1, source_target_pairs={{0,2},{1,3},{2,4},{3,5},{4,6},{5,7},{6,8},{7,9},{8,10},{9,11},{10,... | collective-permute-start | bytes 3538952 | tf_op jit(solution)/shard_map/ppermute | solution.py:220
  12.1 8.6 %collective-permute-start.3 = (bf16[2,192,1536]{2,1,0:T(8,128)(2,1)S(1)}, bf16[2,192,1536]{2,1,0:T(8,128)(2,1)S(1)}, u32[]{:S(2)}, u32[]{:S(2)}) collective-permute-start(bf16[2,192,1536]{2,1,0:T(8,128)(2,1)S(1)} %constant_dynamic-update-slice_fusion.refs_0_), channel_id=1, source_target_pairs={{0,14},{1,15},{2,0},{3,1},{4,2},{5,3},{6,4},{7,5},{8,6},{9,7},{10,... | collective-permute-start | bytes 3538952 | tf_op jit(solution)/shard_map/ppermute | solution.py:220
  20.8 3.9 %shard_map.73 = (bf16[256,1792]{1,0:T(8,128)(2,1)}, f32[128,1536]{1,0:T(8,128)S(1)}, bf16[128,256]{1,0:T(8,128)(2,1)S(1)}, bf16[128,256]{1,0:T(8,128)(2,1)S(1)},...) custom-call(bf16[128,1536]{1,0:T(8,128)(2,1)S(1)} %bitcast.18, ...), custom_call_target="tpu_custom_call" | custom-call | flops 20000000000 | bytes 2655232 | tf_op jit(solution)/shard_map/pallas_call | solution.py:28
  24.8 1.0 copy-done.1
  25.7 18.0 %collective-permute-done.2.refs_1_ = bf16[2,192,1536]{2,1,0:T(8,128)(2,1)S(1)} collective-permute-done((bf16[2,192,1536]{2,1,0:T(8,128)(2,1)S(1)}, bf16[2,192,1536]{2,1,0:T(8,128)(2,1)S(1)}, u32[]{:S(2)}, u32[]{:S(2)}) %collective-permute-start.2) | collective-permute-done | bytes 1179680 | tf_op jit(solution)/shard_map/ppermute | solution.py:220
  43.7 1.2 collective-permute-done.3.refs_2_
  44.9 10.2 %all-to-all-start = ((bf16[32,8,1792]{2,1,0:T(8,128)(2,1)}), bf16[32,8,1792]{2,1,0:T(8,128)(2,1)S(1)}, u32[]{:S(2)}, u32[]{:S(2)}) async-start(bf16[32,8,1792]{2,1,0:T(8,128)(2,1)} %bitcast.6), calls=%async_computation | async-start | bytes 1835008 | tf_op jit(solution)/shard_map/all_to_all | solution.py:233
  55.0 5.6 %collective-permute-start.6 = (bf16[2,192,1536]{2,1,0:T(8,128)(2,1)S(1)}, bf16[2,192,1536]{2,1,0:T(8,128)(2,1)}, u32[]{:S(2)}, u32[]{:S(2)}) collective-permute-start(bf16[2,192,1536]{2,1,0:T(8,128)(2,1)S(1)} %collective-permute-done.3.refs_2_), channel_id=1, source_target_pairs={{0,14},{1,15},{2,0},{3,1},{4,2},{5,3},{6,4},{7,5},{8,6},{9,7},{10,... | collective-permute-start | bytes 3538952 | tf_op jit(solution)/shard_map/ppermute | solution.py:225
  60.7 1.0 copy-done.8
  61.7 1.9 %collective-permute-start.5 = (bf16[2,192,1536]{2,1,0:T(8,128)(2,1)S(1)}, bf16[2,192,1536]{2,1,0:T(8,128)(2,1)}, u32[]{:S(2)}, u32[]{:S(2)}) collective-permute-start(bf16[2,192,1536]{2,1,0:T(8,128)(2,1)S(1)} %collective-permute-done.2.refs_1_), channel_id=1, source_target_pairs={{0,2},{1,3},{2,4},{3,5},{4,6},{5,7},{6,8},{7,9},{8,10},{9,11},{10,... | collective-permute-start | bytes 3538952 | tf_op jit(solution)/shard_map/ppermute | solution.py:225
  63.6 19.7 %collective-permute-done.6.refs_4_ = bf16[2,192,1536]{2,1,0:T(8,128)(2,1)} collective-permute-done((bf16[2,192,1536]{2,1,0:T(8,128)(2,1)S(1)}, bf16[2,192,1536]{2,1,0:T(8,128)(2,1)}, u32[]{:S(2)}, u32[]{:S(2)}) %collective-permute-start.6) | collective-permute-done | bytes 1179680 | tf_op jit(solution)/shard_map/ppermute | solution.py:225
  83.3 5.7 %collective-permute-start.8 = (bf16[2,192,1536]{2,1,0:T(8,128)(2,1)}, bf16[2,192,1536]{2,1,0:T(8,128)(2,1)S(1)}, u32[]{:S(2)}, u32[]{:S(2)}) collective-permute-start(bf16[2,192,1536]{2,1,0:T(8,128)(2,1)} %collective-permute-done.6.refs_4_), channel_id=1, source_target_pairs={{0,14},{1,15},{2,0},{3,1},{4,2},{5,3},{6,4},{7,5},{8,6},{9,7},{10,... | collective-permute-start | bytes 3538952 | tf_op jit(solution)/shard_map/ppermute | solution.py:226
  89.0 0.7 collective-permute-done.5.refs_3_
  89.8 1.9 %collective-permute-start.7 = (bf16[2,192,1536]{2,1,0:T(8,128)(2,1)}, bf16[2,192,1536]{2,1,0:T(8,128)(2,1)S(1)}, u32[]{:S(2)}, u32[]{:S(2)}) collective-permute-start(bf16[2,192,1536]{2,1,0:T(8,128)(2,1)} %collective-permute-done.5.refs_3_), channel_id=1, source_target_pairs={{0,2},{1,3},{2,4},{3,5},{4,6},{5,7},{6,8},{7,9},{8,10},{9,11},{10,... | collective-permute-start | bytes 3538952 | tf_op jit(solution)/shard_map/ppermute | solution.py:226
  91.7 2.1 %collective-permute-start.4 = (bf16[256,1792]{1,0:T(8,128)(2,1)S(1)}, bf16[256,1792]{1,0:T(8,128)(2,1)S(1)}, u32[]{:S(2)}, u32[]{:S(2)}) collective-permute-start(bf16[256,1792]{1,0:T(8,128)(2,1)S(1)} %bitcast.16), channel_id=1, source_target_pairs={{0,1},{1,0},{2,3},{3,2},{4,5},{5,4},{6,7},{7,6},{8,9},{9,8},{10,11... | collective-permute-start | bytes 2752520 | tf_op jit(solution)/shard_map/ppermute | solution.py:237
  93.8 17.3 %collective-permute-done.8.refs_1_ = bf16[2,192,1536]{2,1,0:T(8,128)(2,1)S(1)} collective-permute-done((bf16[2,192,1536]{2,1,0:T(8,128)(2,1)}, bf16[2,192,1536]{2,1,0:T(8,128)(2,1)S(1)}, u32[]{:S(2)}, u32[]{:S(2)}) %collective-permute-start.8) | collective-permute-done | bytes 1179680 | tf_op jit(solution)/shard_map/ppermute | solution.py:226
  111.1 5.5 %collective-permute-start.10 = (bf16[2,96,1536]{2,1,0:T(8,128)(2,1)S(1)}, bf16[2,96,1536]{2,1,0:T(8,128)(2,1)S(1)}, u32[]{:S(2)}, u32[]{:S(2)}) collective-permute-start(bf16[2,96,1536]{2,1,0:T(8,128)(2,1)S(1)} %slice.25), channel_id=1, source_target_pairs={{0,14},{1,15},{2,0},{3,1},{4,2},{5,3},{6,4},{7,5},{8,6},{9,7},{10,... | collective-permute-start | bytes 1769480 | tf_op jit(solution)/shard_map/ppermute | solution.py:228
  117.1 1.9 %collective-permute-start.9 = (bf16[2,96,1536]{2,1,0:T(8,128)(2,1)S(1)}, bf16[2,96,1536]{2,1,0:T(8,128)(2,1)S(1)}, u32[]{:S(2)}, u32[]{:S(2)}) collective-permute-start(bf16[2,96,1536]{2,1,0:T(8,128)(2,1)S(1)} %slice.24), channel_id=1, source_target_pairs={{0,2},{1,3},{2,4},{3,5},{4,6},{5,7},{6,8},{7,9},{8,10},{9,11},{10,... | collective-permute-start | bytes 1769480 | tf_op jit(solution)/shard_map/ppermute | solution.py:228
  119.0 1.3 copy-done.9
  120.3 7.7 %shard_map.74 = (bf16[576,1536]{1,0:T(8,128)(2,1)}, f32[576,1536]{1,0:T(8,128)}) custom-call(bf16[256,1792]{1,0:T(8,128)(2,1)S(1)} %bitcast.17, bf16[256,1792]{1,0:T(8,128)(2,1)S(1)} %collective-permute-done.4.other_ref, bf16[2,192,1536]{2,1,0:T(8,128)(2,1)S(1)} %copy-done.4, bf16[2,192,1536]{2,1,0:T(8,128)(2,1)S(1)} %copy-done.7, ...), custom_call_target="tpu_custom_call" | custom-call | flops 3397386240 | bytes 13041664 | tf_op jit(solution)/shard_map/pallas_call | solution.py:28
  128.0 1.5 copy-done
  129.5 5.8 %shard_map.75.old_ref = f32[576,1536]{1,0:T(8,128)} custom-call(bf16[576,1536]{1,0:T(8,128)(2,1)S(1)} %copy-done, f32[576,1536]{1,0:T(8,128)} %get-tuple-element.23.old_ref, bf16[2,192,1536]{2,1,0:T(8,128)(2,1)S(1)} %collective-permute-done.7.refs_0_, bf16[2,192,1536]{2,1,0:T(8,128)(2,1)S(1)} %collective-permute-done.8.refs_1_), custom_call_target="tpu_custom_call", output_to_operand_aliasing={{}: (1, {})} | custom-call | flops 1358954496 | bytes 11206656 | tf_op jit(solution)/shard_map/pallas_call | solution.py:28
  135.3 4.0 %shard_map.76 = (f32[288,1536]{1,0:T(8,128)S(1)}, bf16[288,1536]{1,0:T(8,128)(2,1)S(1)}) custom-call(bf16[576,1536]{1,0:T(8,128)(2,1)S(1)} %copy-done, f32[576,1536]{1,0:T(8,128)} %shard_map.75.old_ref, bf16[2,96,1536]{2,1,0:T(8,128)(2,1)S(1)} %collective-permute-done.9.refs_0_, bf16[2,96,1536]{2,1,0:T(8,128)(2,1)S(1)} %collective-permute-done.10.refs_1_), custom_call_target="tpu_custom_call" | custom-call | flops 679477248 | bytes 9142272 | tf_op jit(solution)/shard_map/pallas_call | solution.py:28
  139.3 1.9 %collective-permute-start.11 = (bf16[288,1536]{1,0:T(8,128)(2,1)S(1)}, bf16[288,1536]{1,0:T(8,128)(2,1)S(1)}, u32[]{:S(2)}, u32[]{:S(2)}) collective-permute-start(bf16[288,1536]{1,0:T(8,128)(2,1)S(1)} %get-tuple-element.25), channel_id=1, source_target_pairs={{0,1},{1,0},{2,3},{3,2},{4,5},{5,4},{6,7},{7,6},{8,9},{9,8},{10,11... | collective-permute-start | bytes 2654216 | tf_op jit(solution)/shard_map/ppermute | solution.py:256
  141.2 2.4 %collective-permute-done.11.other_ref = bf16[288,1536]{1,0:T(8,128)(2,1)S(1)} collective-permute-done((bf16[288,1536]{1,0:T(8,128)(2,1)S(1)}, bf16[288,1536]{1,0:T(8,128)(2,1)S(1)}, u32[]{:S(2)}, u32[]{:S(2)}) %collective-permute-start.11) | collective-permute-done | bytes 884768 | tf_op jit(solution)/shard_map/ppermute | solution.py:256
  143.6 0.6 shard_map.77
  144.2 35.9 %all_to_all.10 = bf16[32,8,1792]{2,1,0:T(8,128)(2,1)S(1)} all-to-all(bf16[32,8,1792]{2,1,0:T(8,128)(2,1)S(1)} %bitcast.14), channel_id=1, replica_groups=mesh['expert'=32,'dp'=16] {'expert'}, dimensions={0} | all-to-all | bytes 1835008 | tf_op jit(solution)/shard_map/all_to_all | solution.py:233
  180.1 1.3 shard_map.78
  (37 shorter events, 0.6 us)
Async XLA Ops:
  0.0 5.2 %copy-start.13 = (bf16[1,192,1536]{2,1,0:T(8,128)(2,1)S(1)}, bf16[1,192,1536]{2,1,0:T(8,128)(2,1)}, u32[]{:S(2)}) copy-start(bf16[1,192,1536]{2,1,0:T(8,128)(2,1)} %param.12) | copy-start | bytes 1769476
  0.9 19.8 %collective-permute-start = (bf16[16,1536]{1,0:T(8,128)(2,1)S(1)}, bf16[16,1536]{1,0:T(8,128)(2,1)S(1)}, u32[]{:S(2)}, u32[]{:S(2)}) collective-permute-start(bf16[16,1536]{1,0:T(8,128)(2,1)S(1)} %get-tuple-element.32), channel_id=1, source_target_pairs={{0,1},{1,2},{2,3},{3,4},{4,5},{5,6},{6,7},{7,8},{8,9},{9,10},{10,1... | collective-permute-start | bytes 147464 | tf_op jit(solution)/shard_map/ppermute | solution.py:216
  2.6 18.1 %copy-start.14 = (bf16[1536]{0:T(1024)(128)(2,1)S(1)}, bf16[1536]{0:T(1024)(128)(2,1)}, u32[]{:S(2)}) copy-start(bf16[1536]{0:T(1024)(128)(2,1)} %param.9) | copy-start | bytes 9220
  2.6 18.1 %copy-start.5 = (bf16[1,128,1536]{2,1,0:T(8,128)(2,1)S(1)}, bf16[1,128,1536]{2,1,0:T(8,128)(2,1)}, u32[]{:S(2)}) copy-start(bf16[1,128,1536]{2,1,0:T(8,128)(2,1)} %param.7) | copy-start | bytes 1179652
  2.7 18.1 %copy-start.10 = (bf16[31,1536]{1,0:T(8,128)(2,1)S(1)}, bf16[31,1536]{1,0:T(8,128)(2,1)}, u32[]{:S(2)}) copy-start(bf16[31,1536]{1,0:T(8,128)(2,1)} %kernel_ref.1) | copy-start | bytes 285700
  2.7 18.1 %copy-start.11 = (bf16[1536,32]{0,1:T(8,128)(2,1)S(1)}, bf16[1536,32]{0,1:T(8,128)(2,1)}, u32[]{:S(2)}) copy-start(bf16[1536,32]{0,1:T(8,128)(2,1)} %param.10) | copy-start | bytes 294916
  2.7 18.1 %copy-start.12 = (s32[1,128,2]{1,2,0:T(2,128)S(1)}, s32[1,128,2]{1,2,0:T(2,128)}, u32[]{:S(2)}) copy-start(s32[1,128,2]{1,2,0:T(2,128)} %param.13) | copy-start | bytes 3076
  2.7 18.1 %collective-permute-start.1 = (bf16[16,1536]{1,0:T(8,128)(2,1)S(1)}, bf16[16,1536]{1,0:T(8,128)(2,1)S(1)}, u32[]{:S(2)}, u32[]{:S(2)}) collective-permute-start(bf16[16,1536]{1,0:T(8,128)(2,1)S(1)} %get-tuple-element.31), channel_id=1, source_target_pairs={{1,0},{2,1},{3,2},{4,3},{5,4},{6,5},{7,6},{8,7},{9,8},{10,9},{11,1... | collective-permute-start | bytes 147464 | tf_op jit(solution)/shard_map/ppermute | solution.py:217
  5.3 19.5 %copy-start.3 = (bf16[2,192,1536]{2,1,0:T(8,128)(2,1)}, bf16[2,192,1536]{2,1,0:T(8,128)(2,1)S(1)}, u32[]{:S(2)}) copy-start(bf16[2,192,1536]{2,1,0:T(8,128)(2,1)S(1)} %constant_dynamic-update-slice_fusion.refs_0_) | copy-start | bytes 3538948
  5.3 38.4 %collective-permute-start.2 = (bf16[2,192,1536]{2,1,0:T(8,128)(2,1)S(1)}, bf16[2,192,1536]{2,1,0:T(8,128)(2,1)S(1)}, u32[]{:S(2)}, u32[]{:S(2)}) collective-permute-start(bf16[2,192,1536]{2,1,0:T(8,128)(2,1)S(1)} %constant_dynamic-update-slice_fusion.refs_0_), channel_id=1, source_target_pairs={{0,2},{1,3},{2,4},{3,5},{4,6},{5,7},{6,8},{7,9},{8,10},{9,11},{10,... | collective-permute-start | bytes 3538952 | tf_op jit(solution)/shard_map/ppermute | solution.py:220
  12.1 32.7 %collective-permute-start.3 = (bf16[2,192,1536]{2,1,0:T(8,128)(2,1)S(1)}, bf16[2,192,1536]{2,1,0:T(8,128)(2,1)S(1)}, u32[]{:S(2)}, u32[]{:S(2)}) collective-permute-start(bf16[2,192,1536]{2,1,0:T(8,128)(2,1)S(1)} %constant_dynamic-update-slice_fusion.refs_0_), channel_id=1, source_target_pairs={{0,14},{1,15},{2,0},{3,1},{4,2},{5,3},{6,4},{7,5},{8,6},{9,7},{10,... | collective-permute-start | bytes 3538952 | tf_op jit(solution)/shard_map/ppermute | solution.py:220
  24.8 1.0 copy-start.1
  43.7 45.3 %copy-start.6 = (bf16[2,192,1536]{2,1,0:T(8,128)(2,1)}, bf16[2,192,1536]{2,1,0:T(8,128)(2,1)S(1)}, u32[]{:S(2)}) copy-start(bf16[2,192,1536]{2,1,0:T(8,128)(2,1)S(1)} %collective-permute-done.2.refs_1_) | copy-start | bytes 3538948
  44.9 46.8 %all-to-all-start = ((bf16[32,8,1792]{2,1,0:T(8,128)(2,1)}), bf16[32,8,1792]{2,1,0:T(8,128)(2,1)S(1)}, u32[]{:S(2)}, u32[]{:S(2)}) async-start(bf16[32,8,1792]{2,1,0:T(8,128)(2,1)} %bitcast.6), calls=%async_computation | async-start | bytes 1835008 | tf_op jit(solution)/shard_map/all_to_all | solution.py:233
  55.0 28.3 %collective-permute-start.6 = (bf16[2,192,1536]{2,1,0:T(8,128)(2,1)S(1)}, bf16[2,192,1536]{2,1,0:T(8,128)(2,1)}, u32[]{:S(2)}, u32[]{:S(2)}) collective-permute-start(bf16[2,192,1536]{2,1,0:T(8,128)(2,1)S(1)} %collective-permute-done.3.refs_2_), channel_id=1, source_target_pairs={{0,14},{1,15},{2,0},{3,1},{4,2},{5,3},{6,4},{7,5},{8,6},{9,7},{10,... | collective-permute-start | bytes 3538952 | tf_op jit(solution)/shard_map/ppermute | solution.py:225
  60.6 1.0 copy-start.8
  61.7 28.1 %collective-permute-start.5 = (bf16[2,192,1536]{2,1,0:T(8,128)(2,1)S(1)}, bf16[2,192,1536]{2,1,0:T(8,128)(2,1)}, u32[]{:S(2)}, u32[]{:S(2)}) collective-permute-start(bf16[2,192,1536]{2,1,0:T(8,128)(2,1)S(1)} %collective-permute-done.2.refs_1_), channel_id=1, source_target_pairs={{0,2},{1,3},{2,4},{3,5},{4,6},{5,7},{6,8},{7,9},{8,10},{9,11},{10,... | collective-permute-start | bytes 3538952 | tf_op jit(solution)/shard_map/ppermute | solution.py:225
  83.3 27.8 %collective-permute-start.8 = (bf16[2,192,1536]{2,1,0:T(8,128)(2,1)}, bf16[2,192,1536]{2,1,0:T(8,128)(2,1)S(1)}, u32[]{:S(2)}, u32[]{:S(2)}) collective-permute-start(bf16[2,192,1536]{2,1,0:T(8,128)(2,1)} %collective-permute-done.6.refs_4_), channel_id=1, source_target_pairs={{0,14},{1,15},{2,0},{3,1},{4,2},{5,3},{6,4},{7,5},{8,6},{9,7},{10,... | collective-permute-start | bytes 3538952 | tf_op jit(solution)/shard_map/ppermute | solution.py:226
  89.8 27.3 %collective-permute-start.7 = (bf16[2,192,1536]{2,1,0:T(8,128)(2,1)}, bf16[2,192,1536]{2,1,0:T(8,128)(2,1)S(1)}, u32[]{:S(2)}, u32[]{:S(2)}) collective-permute-start(bf16[2,192,1536]{2,1,0:T(8,128)(2,1)} %collective-permute-done.5.refs_3_), channel_id=1, source_target_pairs={{0,2},{1,3},{2,4},{3,5},{4,6},{5,7},{6,8},{7,9},{8,10},{9,11},{10,... | collective-permute-start | bytes 3538952 | tf_op jit(solution)/shard_map/ppermute | solution.py:226
  91.7 27.3 %copy-start.4 = (bf16[2,192,1536]{2,1,0:T(8,128)(2,1)S(1)}, bf16[2,192,1536]{2,1,0:T(8,128)(2,1)}, u32[]{:S(2)}) copy-start(bf16[2,192,1536]{2,1,0:T(8,128)(2,1)} %copy-done.3) | copy-start | bytes 3538948
  91.7 27.3 %copy-start.7 = (bf16[2,192,1536]{2,1,0:T(8,128)(2,1)S(1)}, bf16[2,192,1536]{2,1,0:T(8,128)(2,1)}, u32[]{:S(2)}) copy-start(bf16[2,192,1536]{2,1,0:T(8,128)(2,1)} %copy-done.6) | copy-start | bytes 3538948
  91.7 27.3 %collective-permute-start.4 = (bf16[256,1792]{1,0:T(8,128)(2,1)S(1)}, bf16[256,1792]{1,0:T(8,128)(2,1)S(1)}, u32[]{:S(2)}, u32[]{:S(2)}) collective-permute-start(bf16[256,1792]{1,0:T(8,128)(2,1)S(1)} %bitcast.16), channel_id=1, source_target_pairs={{0,1},{1,0},{2,3},{3,2},{4,5},{5,4},{6,7},{7,6},{8,9},{9,8},{10,11... | collective-permute-start | bytes 2752520 | tf_op jit(solution)/shard_map/ppermute | solution.py:237
  111.1 24.2 %collective-permute-start.10 = (bf16[2,96,1536]{2,1,0:T(8,128)(2,1)S(1)}, bf16[2,96,1536]{2,1,0:T(8,128)(2,1)S(1)}, u32[]{:S(2)}, u32[]{:S(2)}) collective-permute-start(bf16[2,96,1536]{2,1,0:T(8,128)(2,1)S(1)} %slice.25), channel_id=1, source_target_pairs={{0,14},{1,15},{2,0},{3,1},{4,2},{5,3},{6,4},{7,5},{8,6},{9,7},{10,... | collective-permute-start | bytes 1769480 | tf_op jit(solution)/shard_map/ppermute | solution.py:228
  117.1 18.2 %collective-permute-start.9 = (bf16[2,96,1536]{2,1,0:T(8,128)(2,1)S(1)}, bf16[2,96,1536]{2,1,0:T(8,128)(2,1)S(1)}, u32[]{:S(2)}, u32[]{:S(2)}) collective-permute-start(bf16[2,96,1536]{2,1,0:T(8,128)(2,1)S(1)} %slice.24), channel_id=1, source_target_pairs={{0,2},{1,3},{2,4},{3,5},{4,6},{5,7},{6,8},{7,9},{8,10},{9,11},{10,... | collective-permute-start | bytes 1769480 | tf_op jit(solution)/shard_map/ppermute | solution.py:228
  119.0 1.3 copy-start.9
  128.0 1.5 copy-start
  139.3 4.3 %collective-permute-start.11 = (bf16[288,1536]{1,0:T(8,128)(2,1)S(1)}, bf16[288,1536]{1,0:T(8,128)(2,1)S(1)}, u32[]{:S(2)}, u32[]{:S(2)}) collective-permute-start(bf16[288,1536]{1,0:T(8,128)(2,1)S(1)} %get-tuple-element.25), channel_id=1, source_target_pairs={{0,1},{1,0},{2,3},{3,2},{4,5},{5,4},{6,7},{7,6},{8,9},{9,8},{10,11... | collective-permute-start | bytes 2654216 | tf_op jit(solution)/shard_map/ppermute | solution.py:256
  144.2 35.9 %copy-start.2 = (f32[128,1536]{1,0:T(8,128)S(1)}, f32[128,1536]{1,0:T(8,128)}, u32[]{:S(2)}) copy-start(f32[128,1536]{1,0:T(8,128)} %copy-done.1) | copy-start | bytes 2359300

commit v2 on v1

--- a/solution.py
+++ b/solution.py
@@ -23,7 +23,7 @@
     return lax.broadcasted_iota(i32, shape, dim)
 
 
-def call(kernel, outs, args, flops, scratch=(), aliases={}, limit=48 << 20):
+def call(kernel, outs, args, flops, scratch=(), aliases={}, limit=20 << 20):
     moved = sum(x.size * x.dtype.itemsize for x in (*args, *outs))
     return pl.pallas_call(
         kernel,
@@ -126,8 +126,10 @@
 
 
 def ffn(rows, blocks):
-    first = jnp.concatenate([b[0] for b in blocks], axis=0)
-    second = jnp.concatenate([b[1] for b in blocks], axis=0)
+    whole = [b for b in blocks if len(b.shape) == 3]
+    split = [b for b in blocks if len(b.shape) == 2]
+    first = jnp.concatenate([b[0] for b in whole] + [b[...] for b in split[::2]], axis=0)
+    second = jnp.concatenate([b[1] for b in whole] + [b[...] for b in split[1::2]], axis=0)
     preact = lax.dot_general(rows, first, TRANSPOSED, preferred_element_type=f32)
     hidden = (preact / (1.0 + jnp.exp(-preact))).astype(bf16)
     return hidden, second
@@ -216,16 +218,19 @@
     low = lax.ppermute(frames[tok - HALO :], "dp", [(i, i + 1) for i in range(dp - 1)])
     high = lax.ppermute(frames[:HALO], "dp", [(i + 1, i) for i in range(dp - 1)])
 
+    units = w_in.shape[1]
     own = jnp.concatenate([w_in, w_out], axis=0)
     a1, b1 = lax.ppermute(own, "dp", up), lax.ppermute(own, "dp", down)
+
+    def step(ups, downs):
+        moved = [(lax.ppermute(a, "dp", up), lax.ppermute(b, "dp", down)) for a, b in zip(ups, downs)]
+        return [m[0] for m in moved], [m[1] for m in moved]
+
+    a2, b2 = step([a1[0], a1[1]], [b1[0], b1[1]])
+    a3, b3 = step(a2, b2)
     sent, residual, *weights = front(
         frames, low, high, conv_kernel, norm_gain[None], router.T, routes[0].T
     )
-    sent, a1, b1 = lax.optimization_barrier((sent, a1, b1))
-    a2, b2 = lax.ppermute(a1, "dp", up), lax.ppermute(b1, "dp", down)
-    a3, b3 = lax.ppermute(a2, "dp", up), lax.ppermute(b2, "dp", down)
-    half = own.shape[1] // 2
-    a4, b4 = lax.ppermute(a3[:, :half], "dp", up), lax.ppermute(b3[:, half:], "dp", down)
     assert chips == 8
 
     def exchange(v):
@@ -237,20 +242,22 @@
     other = lax.ppermute(mine, "dp", sibling)
     count = experts * (MAIN + 1)
     flops = lambda units: 2 * 2 * 2 * count * units * features
-    units = own.shape[1]
     rows, total = call(
         begin_kernel,
         (shape((2 * count, features), bf16), shape((2 * count, features), f32)),
-        (mine, other, own, a1, b1, a2, b2),
+        (mine, other, own, a1, b1, *a2, *b2),
         flops(5 * units),
     )
+    total, a3[0], b3[0] = lax.optimization_barrier((total, a3[0], b3[0]))
+    half = units // 2
+    a4, b4 = step([a[:half] for a in a3], [b[half:] for b in b3])
     (total,) = call(
-        more_kernel, (shape(total.shape, f32),), (rows, total, a3, b3), flops(2 * units), aliases={1: 0}
+        more_kernel, (shape(total.shape, f32),), (rows, total, *a3, *b3), flops(2 * units), aliases={1: 0}
     )
     kept, gone = call(
         end_kernel,
         (shape((count, features), f32), shape((count, features), bf16)),
-        (rows, total, a4, b4),
+        (rows, total, *a4, *b4),
         flops(units),
     )
     came = lax.ppermute(gone, "dp", sibling)

time: 182 us -> 164 us (0.901)
  waiting for transfers between devices: 59.7 us -> 35.8 us
  starting transfers between devices: 55.2 us -> 73.3 us
  Pallas kernels: 23.4 us -> 15.1 us
  blocking collectives: 35.9 us -> 31.1 us
    ppermute x6 -> x12, waiting for transfers between devices: 38.2 us -> 18.1 us  [the longest x6 12.8 us: step(): lax.ppermute(a, 'dp', up)]
    ppermute x6 -> x12, starting transfers between devices: 22.5 us -> 40.8 us  [the longest x6 29 us: step(): lax.ppermute(b, 'dp', down)]
    ppermute x2, waiting for transfers between devices: 19.1 us -> 8.1 us  [shards(): a1, b1 = (lax.ppermute(own, 'dp', up), lax.ppermute(own, 'dp', down))]
    pallas_call x6, Pallas kernels: 23.4 us -> 15.1 us  [call(): pl.pallas_call(kernel, out_shape=outs, in_specs=[pl.BlockSpec(memory_spac...]
    all_to_all x1, waiting for transfers between devices: 0.01 us -> 7.18 us  [exchange(): lax.all_to_all(parts, 'expert', split_axis=0, concat_axis=0, tiled=True)]
    all_to_all x1, blocking collectives: 35.9 us -> 31.1 us  [exchange(): lax.all_to_all(parts, 'expert', split_axis=0, concat_axis=0, tiled=True)]
    squeeze x0 -> x2, local copies, waits for them, and re-layouts: none -> 2.18 us  [shards(): a2, b2 = step([a1[0], a1[1]], [b1[0], b1[1]])]
    unnamed x31 -> x19, local copies, waits for them, and re-layouts: 5.88 us -> 3.76 us
  transfers between devices with their start and end apart: 13 -> 19, of which waited for: 7 -> 6; matrix products, arithmetic and copies ran while one was open for 1% -> 3% of each run, Pallas kernels for 10% -> 7%
where the time goes in v2:
time: 164 us
  starting transfers between devices  73.3 us (45%)
  waiting for transfers between devices  35.8 us (22%)
  blocking collectives  31.1 us (19%)
  Pallas kernels  15.1 us (9%)
  local copies, waits for them, and re-layouts  7.81 us (5%)
    all_to_all x1, blocking collectives, exchange(): lax.all_to_all(parts, 'expert', split_axis=0, concat_axis=0, tiled=True)  31.1 us
    ppermute x6, starting transfers between devices, step(): lax.ppermute(b, 'dp', down)  29 us
    ppermute x2, starting transfers between devices, shards(): a1, b1 = (lax.ppermute(own, 'dp', up), lax.ppermute(own, 'dp', down))  15.4 us
    pallas_call x6, Pallas kernels, call(): pl.pallas_call(kernel, out_shape=outs, in_specs=[pl.BlockSpec(memory_spac...  15.1 us
    ppermute x6, waiting for transfers between devices, step(): lax.ppermute(a, 'dp', up)  12.8 us
    ppermute x6, starting transfers between devices, step(): lax.ppermute(a, 'dp', up)  11.8 us
    all_to_all x1, starting transfers between devices, exchange(): lax.all_to_all(parts, 'expert', split_axis=0, concat_axis=0, tiled=True)  10.2 us
    ppermute x2, waiting for transfers between devices, shards(): a1, b1 = (lax.ppermute(own, 'dp', up), lax.ppermute(own, 'dp', down))  8.1 us
  transfers between devices with their start and end apart: 19, of which 6 were waited for; matrix products, arithmetic and copies ran while one was open for 3% of the time, Pallas kernels for 7%

profile of v2, /device:TPU:8, one launch (start us, length us, event | category | flops | bytes accessed | tf_op | source)
XLA Modules:
  0.0 163.6 jit_solution(3687872090472023077)
XLA Ops:
  0.9 1.7 %collective-permute-start = (bf16[16,1536]{1,0:T(8,128)(2,1)S(1)}, bf16[16,1536]{1,0:T(8,128)(2,1)S(1)}, u32[]{:S(2)}, u32[]{:S(2)}) collective-permute-start(bf16[16,1536]{1,0:T(8,128)(2,1)S(1)} %get-tuple-element.36), channel_id=1, source_target_pairs={{0,1},{1,2},{2,3},{3,4},{4,5},{5,6},{6,7},{7,8},{8,9},{9,10},{10,1... | collective-permute-start | bytes 147464 | tf_op jit(solution)/shard_map/ppermute | solution.py:218
  2.7 1.4 collective-permute-start.1
  4.1 1.9 %constant_dynamic-update-slice_fusion.1 = bf16[2,192,1536]{2,1,0:T(8,128)(2,1)} fusion(bf16[1,192,1536]{2,1,0:T(8,128)(2,1)} %param.11), kind=kLoop, calls=%fused_computation.7 | loop fusion | bytes 1179648
  6.9 6.8 %collective-permute-start.3 = (bf16[2,192,1536]{2,1,0:T(8,128)(2,1)}, bf16[2,192,1536]{2,1,0:T(8,128)(2,1)S(1)}, u32[]{:S(2)}, u32[]{:S(2)}) collective-permute-start(bf16[2,192,1536]{2,1,0:T(8,128)(2,1)} %constant_dynamic-update-slice_fusion.refs_0_), channel_id=1, source_target_pairs={{0,2},{1,3},{2,4},{3,5},{4,6},{5,7},{6,8},{7,9},{8,10},{9,11},{10,... | collective-permute-start | bytes 3538952 | tf_op jit(solution)/shard_map/ppermute | solution.py:223
  13.7 8.6 %collective-permute-start.4 = (bf16[2,192,1536]{2,1,0:T(8,128)(2,1)}, bf16[2,192,1536]{2,1,0:T(8,128)(2,1)S(1)}, u32[]{:S(2)}, u32[]{:S(2)}) collective-permute-start(bf16[2,192,1536]{2,1,0:T(8,128)(2,1)} %constant_dynamic-update-slice_fusion.refs_0_), channel_id=1, source_target_pairs={{0,14},{1,15},{2,0},{3,1},{4,2},{5,3},{6,4},{7,5},{8,6},{9,7},{10,... | collective-permute-start | bytes 3538952 | tf_op jit(solution)/shard_map/ppermute | solution.py:223
  22.4 3.0 %shard_map.73 = (bf16[256,1792]{1,0:T(8,128)(2,1)S(1)}, f32[128,1536]{1,0:T(8,128)S(1)}, bf16[128,256]{1,0:T(8,128)(2,1)S(1)}, bf16[128,256]{1,0:T(8,128)(2,1)S(...) custom-call(bf16[128,1536]{1,0:T(8,128)(2,1)S(1)} %bitcast.27, ...), custom_call_target="tpu_custom_call" | custom-call | flops 20000000000 | bytes 2655232 | tf_op jit(solution)/shard_map/pallas_call | solution.py:28
  27.2 10.2 %all-to-all-start = ((bf16[32,8,1792]{2,1,0:T(8,128)(2,1)}), bf16[32,8,1792]{2,1,0:T(8,128)(2,1)S(1)}, u32[]{:S(2)}, u32[]{:S(2)}) async-start(bf16[32,8,1792]{2,1,0:T(8,128)(2,1)} %bitcast.26), calls=%async_computation | async-start | bytes 1835008 | tf_op jit(solution)/shard_map/all_to_all | solution.py:238
  37.4 8.1 %collective-permute-done.3.refs_1_ = bf16[2,192,1536]{2,1,0:T(8,128)(2,1)S(1)} collective-permute-done((bf16[2,192,1536]{2,1,0:T(8,128)(2,1)}, bf16[2,192,1536]{2,1,0:T(8,128)(2,1)S(1)}, u32[]{:S(2)}, u32[]{:S(2)}) %collective-permute-start.3) | collective-permute-done | bytes 1179680 | tf_op jit(solution)/shard_map/ppermute | solution.py:223
  46.6 1.9 %collective-permute-start.6 = (bf16[192,1536]{1,0:T(8,128)(2,1)}, bf16[192,1536]{1,0:T(8,128)(2,1)}, u32[]{:S(2)}, u32[]{:S(2)}) collective-permute-start(bf16[192,1536]{1,0:T(8,128)(2,1)} %get-tuple-element.33), channel_id=1, source_target_pairs={{0,2},{1,3},{2,4},{3,5},{4,6},{5,7},{6,8},{7,9},{8,10},{9,11},{10,... | collective-permute-start | bytes 1769480 | tf_op jit(solution)/shard_map/ppermute | solution.py:226
  49.6 5.1 %collective-permute-start.8 = (bf16[192,1536]{1,0:T(8,128)(2,1)}, bf16[192,1536]{1,0:T(8,128)(2,1)}, u32[]{:S(2)}, u32[]{:S(2)}) collective-permute-start(bf16[192,1536]{1,0:T(8,128)(2,1)} %get-tuple-element.31), channel_id=1, source_target_pairs={{0,14},{1,15},{2,0},{3,1},{4,2},{5,3},{6,4},{7,5},{8,6},{9,7},{10,... | collective-permute-start | bytes 1769480 | tf_op jit(solution)/shard_map/ppermute | solution.py:226
  54.8 7.2 %all-to-all-done = bf16[32,8,1792]{2,1,0:T(8,128)(2,1)S(1)} async-done(((bf16[32,8,1792]{2,1,0:T(8,128)(2,1)}), bf16[32,8,1792]{2,1,0:T(8,128)(2,1)S(1)}, u32[]{:S(2)}, u32[]{:S(2)}) %all-to-all-start) | async-done | bytes 917536 | tf_op jit(solution)/shard_map/all_to_all | solution.py:238
  61.9 1.9 %collective-permute-start.2 = (bf16[256,1792]{1,0:T(8,128)(2,1)S(1)}, bf16[256,1792]{1,0:T(8,128)(2,1)S(1)}, u32[]{:S(2)}, u32[]{:S(2)}) collective-permute-start(bf16[256,1792]{1,0:T(8,128)(2,1)S(1)} %bitcast.24), channel_id=1, source_target_pairs={{0,1},{1,0},{2,3},{3,2},{4,5},{5,4},{6,7},{7,6},{8,9},{9,8},{10,11... | collective-permute-start | bytes 2752520 | tf_op jit(solution)/shard_map/ppermute | solution.py:242
  63.9 3.6 %collective-permute-start.7 = (bf16[192,1536]{1,0:T(8,128)(2,1)}, bf16[192,1536]{1,0:T(8,128)(2,1)S(1)}, u32[]{:S(2)}, u32[]{:S(2)}) collective-permute-start(bf16[192,1536]{1,0:T(8,128)(2,1)} %get-tuple-element.32), channel_id=1, source_target_pairs={{0,14},{1,15},{2,0},{3,1},{4,2},{5,3},{6,4},{7,5},{8,6},{9,7},{10,... | collective-permute-start | bytes 1769480 | tf_op jit(solution)/shard_map/ppermute | solution.py:226
  67.5 2.2 %collective-permute-start.5 = (bf16[192,1536]{1,0:T(8,128)(2,1)}, bf16[192,1536]{1,0:T(8,128)(2,1)S(1)}, u32[]{:S(2)}, u32[]{:S(2)}) collective-permute-start(bf16[192,1536]{1,0:T(8,128)(2,1)} %get-tuple-element.34), channel_id=1, source_target_pairs={{0,2},{1,3},{2,4},{3,5},{4,6},{5,7},{6,8},{7,9},{8,10},{9,11},{10,... | collective-permute-start | bytes 1769480 | tf_op jit(solution)/shard_map/ppermute | solution.py:226
  69.7 1.9 %collective-permute-start.11 = (bf16[192,1536]{1,0:T(8,128)(2,1)}, bf16[192,1536]{1,0:T(8,128)(2,1)S(1)}, u32[]{:S(2)}, u32[]{:S(2)}) collective-permute-start(bf16[192,1536]{1,0:T(8,128)(2,1)} %collective-permute-done.6.refs_4_), channel_id=1, source_target_pairs={{0,2},{1,3},{2,4},{3,5},{4,6},{5,7},{6,8},{7,9},{8,10},{9,11},{10,... | collective-permute-start | bytes 1769480 | tf_op jit(solution)/shard_map/ppermute | solution.py:226
  71.7 5.1 %collective-permute-start.12 = (bf16[192,1536]{1,0:T(8,128)(2,1)}, bf16[192,1536]{1,0:T(8,128)(2,1)S(1)}, u32[]{:S(2)}, u32[]{:S(2)}) collective-permute-start(bf16[192,1536]{1,0:T(8,128)(2,1)} %collective-permute-done.8.refs_6_), channel_id=1, source_target_pairs={{0,14},{1,15},{2,0},{3,1},{4,2},{5,3},{6,4},{7,5},{8,6},{9,7},{10,... | collective-permute-start | bytes 1769480 | tf_op jit(solution)/shard_map/ppermute | solution.py:226
  76.8 5.3 %collective-permute-done.7.refs_5_ = bf16[192,1536]{1,0:T(8,128)(2,1)S(1)} collective-permute-done((bf16[192,1536]{1,0:T(8,128)(2,1)}, bf16[192,1536]{1,0:T(8,128)(2,1)S(1)}, u32[]{:S(2)}, u32[]{:S(2)}) %collective-permute-start.7) | collective-permute-done | bytes 589856 | tf_op jit(solution)/shard_map/ppermute | solution.py:226
  82.1 4.8 %collective-permute-start.10 = (bf16[192,1536]{1,0:T(8,128)(2,1)S(1)}, bf16[192,1536]{1,0:T(8,128)(2,1)S(1)}, u32[]{:S(2)}, u32[]{:S(2)}) collective-permute-start(bf16[192,1536]{1,0:T(8,128)(2,1)S(1)} %collective-permute-done.7.refs_5_), channel_id=1, source_target_pairs={{0,14},{1,15},{2,0},{3,1},{4,2},{5,3},{6,4},{7,5},{8,6},{9,7},{10,... | collective-permute-start | bytes 1769480 | tf_op jit(solution)/shard_map/ppermute | solution.py:226
  87.0 1.9 %collective-permute-start.9 = (bf16[192,1536]{1,0:T(8,128)(2,1)S(1)}, bf16[192,1536]{1,0:T(8,128)(2,1)S(1)}, u32[]{:S(2)}, u32[]{:S(2)}) collective-permute-start(bf16[192,1536]{1,0:T(8,128)(2,1)S(1)} %collective-permute-done.5.refs_3_), channel_id=1, source_target_pairs={{0,2},{1,3},{2,4},{3,5},{4,6},{5,7},{6,8},{7,9},{8,10},{9,11},{10,... | collective-permute-start | bytes 1769480 | tf_op jit(solution)/shard_map/ppermute | solution.py:226
  88.9 10.7 %collective-permute-done.11.refs_1_ = bf16[192,1536]{1,0:T(8,128)(2,1)S(1)} collective-permute-done((bf16[192,1536]{1,0:T(8,128)(2,1)}, bf16[192,1536]{1,0:T(8,128)(2,1)S(1)}, u32[]{:S(2)}, u32[]{:S(2)}) %collective-permute-start.11) | collective-permute-done | bytes 589856 | tf_op jit(solution)/shard_map/ppermute | solution.py:226
  99.6 1.9 %collective-permute-start.14 = (bf16[96,1536]{1,0:T(8,128)(2,1)S(1)}, bf16[96,1536]{1,0:T(8,128)(2,1)S(1)}, u32[]{:S(2)}, u32[]{:S(2)}) collective-permute-start(bf16[96,1536]{1,0:T(8,128)(2,1)S(1)} %slice.52), channel_id=1, source_target_pairs={{0,2},{1,3},{2,4},{3,5},{4,6},{5,7},{6,8},{7,9},{8,10},{9,11},{10,... | collective-permute-start | bytes 884744 | tf_op jit(solution)/shard_map/ppermute | solution.py:226
  101.6 5.1 %collective-permute-start.16 = (bf16[96,1536]{1,0:T(8,128)(2,1)S(1)}, bf16[96,1536]{1,0:T(8,128)(2,1)S(1)}, u32[]{:S(2)}, u32[]{:S(2)}) collective-permute-start(bf16[96,1536]{1,0:T(8,128)(2,1)S(1)} %slice.53), channel_id=1, source_target_pairs={{0,14},{1,15},{2,0},{3,1},{4,2},{5,3},{6,4},{7,5},{8,6},{9,7},{10,... | collective-permute-start | bytes 884744 | tf_op jit(solution)/shard_map/ppermute | solution.py:226
  106.8 5.9 %shard_map.74 = (bf16[576,1536]{1,0:T(8,128)(2,1)S(1)}, f32[576,1536]{1,0:T(8,128)S(1)}) custom-call(bf16[256,1792]{1,0:T(8,128)(2,1)S(1)} %bitcast.25, bf16[256,1792]{1,0:T(8,128)(2,1)S(1)} %collective-permute-done.2.other_ref, bf16[2,192,1536]{2,1,0:T(8,128)(2,1)} %constant_dynamic-update-slice_fusion.refs_0_, ...), custom_call_target="tpu_custom_call" | custom-call | flops 3397386240 | bytes 13041664 | tf_op jit(solution)/shard_map/pallas_call | solution.py:28
  112.7 1.9 %collective-permute-start.13 = (bf16[96,1536]{1,0:T(8,128)(2,1)S(1)}, bf16[96,1536]{1,0:T(8,128)(2,1)S(1)}, u32[]{:S(2)}, u32[]{:S(2)}) collective-permute-start(bf16[96,1536]{1,0:T(8,128)(2,1)S(1)} %slice.44), channel_id=1, source_target_pairs={{0,2},{1,3},{2,4},{3,5},{4,6},{5,7},{6,8},{7,9},{8,10},{9,11},{10,... | collective-permute-start | bytes 884744 | tf_op jit(solution)/shard_map/ppermute | solution.py:226
  114.7 5.1 %collective-permute-start.15 = (bf16[96,1536]{1,0:T(8,128)(2,1)S(1)}, bf16[96,1536]{1,0:T(8,128)(2,1)S(1)}, u32[]{:S(2)}, u32[]{:S(2)}) collective-permute-start(bf16[96,1536]{1,0:T(8,128)(2,1)S(1)} %slice.46), channel_id=1, source_target_pairs={{0,14},{1,15},{2,0},{3,1},{4,2},{5,3},{6,4},{7,5},{8,6},{9,7},{10,... | collective-permute-start | bytes 884744 | tf_op jit(solution)/shard_map/ppermute | solution.py:226
  119.8 2.3 %shard_map.75.old_ref = f32[576,1536]{1,0:T(8,128)S(1)} custom-call(bf16[576,1536]{1,0:T(8,128)(2,1)S(1)} %get-tuple-element.19.rows_ref, f32[576,1536]{1,0:T(8,128)S(1)} %get-tuple-element.21.old_ref, bf16[192,1536]{1,0:T(8,128)(2,1)S(1)} %collective-permute-done.9.refs_0_, ...), custom_call_target="tpu_custom_call", output_to_operand_aliasing={{}: (1, {})} | custom-call | flops 1358954496 | bytes 11206656 | tf_op jit(solution)/shard_map/pallas_call | solution.py:28
  122.1 2.1 %collective-permute-done.13.refs_0_ = bf16[96,1536]{1,0:T(8,128)(2,1)S(1)} collective-permute-done((bf16[96,1536]{1,0:T(8,128)(2,1)S(1)}, bf16[96,1536]{1,0:T(8,128)(2,1)S(1)}, u32[]{:S(2)}, u32[]{:S(2)}) %collective-permute-start.13) | collective-permute-done | bytes 294944 | tf_op jit(solution)/shard_map/ppermute | solution.py:226
  124.2 2.0 %shard_map.76 = (f32[288,1536]{1,0:T(8,128)S(1)}, bf16[288,1536]{1,0:T(8,128)(2,1)S(1)}) custom-call(bf16[576,1536]{1,0:T(8,128)(2,1)S(1)} %get-tuple-element.19.rows_ref, f32[576,1536]{1,0:T(8,128)S(1)} %shard_map.75.old_ref, bf16[96,1536]{1,0:T(8,128)(2,1)S(1)} %collective-permute-done.13.refs_0_, bf16[96,1536]{1,0:T(8,128)(2,1)S(1)} %collective-permute-done.14.refs_1_, ...), custom_call_target="tpu_custom_call" | custom-call | flops 679477248 | bytes 9142272 | tf_op jit(solution)/shard_map/pallas_call | solution.py:28
  126.2 1.9 %collective-permute-start.17 = (bf16[288,1536]{1,0:T(8,128)(2,1)S(1)}, bf16[288,1536]{1,0:T(8,128)(2,1)S(1)}, u32[]{:S(2)}, u32[]{:S(2)}) collective-permute-start(bf16[288,1536]{1,0:T(8,128)(2,1)S(1)} %get-tuple-element.25), channel_id=1, source_target_pairs={{0,1},{1,0},{2,3},{3,2},{4,5},{5,4},{6,7},{7,6},{8,9},{9,8},{10,11... | collective-permute-start | bytes 2654216 | tf_op jit(solution)/shard_map/ppermute | solution.py:263
  128.1 2.4 %collective-permute-done.17.other_ref = bf16[288,1536]{1,0:T(8,128)(2,1)S(1)} collective-permute-done((bf16[288,1536]{1,0:T(8,128)(2,1)S(1)}, bf16[288,1536]{1,0:T(8,128)(2,1)S(1)}, u32[]{:S(2)}, u32[]{:S(2)}) %collective-permute-start.17) | collective-permute-done | bytes 884768 | tf_op jit(solution)/shard_map/ppermute | solution.py:263
  131.1 31.1 %all_to_all.10 = bf16[32,8,1792]{2,1,0:T(8,128)(2,1)S(1)} all-to-all(bf16[32,8,1792]{2,1,0:T(8,128)(2,1)S(1)} %bitcast.22), channel_id=1, replica_groups=mesh['expert'=32,'dp'=16] {'expert'}, dimensions={0} | all-to-all | bytes 1835008 | tf_op jit(solution)/shard_map/all_to_all | solution.py:238
  162.3 1.3 shard_map.78
  (41 shorter events, 6.6 us)
Async XLA Ops:
  0.0 6.0 %copy-start.7 = (bf16[1,192,1536]{2,1,0:T(8,128)(2,1)S(1)}, bf16[1,192,1536]{2,1,0:T(8,128)(2,1)}, u32[]{:S(2)}) copy-start(bf16[1,192,1536]{2,1,0:T(8,128)(2,1)} %param.12) | copy-start | bytes 1769476
  0.9 21.5 %collective-permute-start = (bf16[16,1536]{1,0:T(8,128)(2,1)S(1)}, bf16[16,1536]{1,0:T(8,128)(2,1)S(1)}, u32[]{:S(2)}, u32[]{:S(2)}) collective-permute-start(bf16[16,1536]{1,0:T(8,128)(2,1)S(1)} %get-tuple-element.36), channel_id=1, source_target_pairs={{0,1},{1,2},{2,3},{3,4},{4,5},{5,6},{6,7},{7,8},{8,9},{9,10},{10,1... | collective-permute-start | bytes 147464 | tf_op jit(solution)/shard_map/ppermute | solution.py:218
  2.6 19.7 %copy-start.8 = (bf16[1536]{0:T(1024)(128)(2,1)S(1)}, bf16[1536]{0:T(1024)(128)(2,1)}, u32[]{:S(2)}) copy-start(bf16[1536]{0:T(1024)(128)(2,1)} %param.9) | copy-start | bytes 9220
  2.6 19.7 %copy-start.3 = (bf16[1,128,1536]{2,1,0:T(8,128)(2,1)S(1)}, bf16[1,128,1536]{2,1,0:T(8,128)(2,1)}, u32[]{:S(2)}) copy-start(bf16[1,128,1536]{2,1,0:T(8,128)(2,1)} %param.7) | copy-start | bytes 1179652
  2.7 19.7 %copy-start.4 = (bf16[31,1536]{1,0:T(8,128)(2,1)S(1)}, bf16[31,1536]{1,0:T(8,128)(2,1)}, u32[]{:S(2)}) copy-start(bf16[31,1536]{1,0:T(8,128)(2,1)} %kernel_ref.1) | copy-start | bytes 285700
  2.7 19.7 %copy-start.5 = (bf16[1536,32]{0,1:T(8,128)(2,1)S(1)}, bf16[1536,32]{0,1:T(8,128)(2,1)}, u32[]{:S(2)}) copy-start(bf16[1536,32]{0,1:T(8,128)(2,1)} %param.10) | copy-start | bytes 294916
  2.7 19.7 %copy-start.6 = (s32[1,128,2]{1,2,0:T(2,128)S(1)}, s32[1,128,2]{1,2,0:T(2,128)}, u32[]{:S(2)}) copy-start(s32[1,128,2]{1,2,0:T(2,128)} %param.13) | copy-start | bytes 3076
  2.7 19.7 %collective-permute-start.1 = (bf16[16,1536]{1,0:T(8,128)(2,1)S(1)}, bf16[16,1536]{1,0:T(8,128)(2,1)S(1)}, u32[]{:S(2)}, u32[]{:S(2)}) collective-permute-start(bf16[16,1536]{1,0:T(8,128)(2,1)S(1)} %get-tuple-element.35), channel_id=1, source_target_pairs={{1,0},{2,1},{3,2},{4,3},{5,4},{6,5},{7,6},{8,7},{9,8},{10,9},{11,1... | collective-permute-start | bytes 147464 | tf_op jit(solution)/shard_map/ppermute | solution.py:219
  6.9 38.6 %collective-permute-start.3 = (bf16[2,192,1536]{2,1,0:T(8,128)(2,1)}, bf16[2,192,1536]{2,1,0:T(8,128)(2,1)S(1)}, u32[]{:S(2)}, u32[]{:S(2)}) collective-permute-start(bf16[2,192,1536]{2,1,0:T(8,128)(2,1)} %constant_dynamic-update-slice_fusion.refs_0_), channel_id=1, source_target_pairs={{0,2},{1,3},{2,4},{3,5},{4,6},{5,7},{6,8},{7,9},{8,10},{9,11},{10,... | collective-permute-start | bytes 3538952 | tf_op jit(solution)/shard_map/ppermute | solution.py:223
  13.7 34.8 %collective-permute-start.4 = (bf16[2,192,1536]{2,1,0:T(8,128)(2,1)}, bf16[2,192,1536]{2,1,0:T(8,128)(2,1)S(1)}, u32[]{:S(2)}, u32[]{:S(2)}) collective-permute-start(bf16[2,192,1536]{2,1,0:T(8,128)(2,1)} %constant_dynamic-update-slice_fusion.refs_0_), channel_id=1, source_target_pairs={{0,14},{1,15},{2,0},{3,1},{4,2},{5,3},{6,4},{7,5},{8,6},{9,7},{10,... | collective-permute-start | bytes 3538952 | tf_op jit(solution)/shard_map/ppermute | solution.py:223
  25.4 0.9 copy-start
  26.4 0.9 copy-start.1
  27.2 34.7 %all-to-all-start = ((bf16[32,8,1792]{2,1,0:T(8,128)(2,1)}), bf16[32,8,1792]{2,1,0:T(8,128)(2,1)S(1)}, u32[]{:S(2)}, u32[]{:S(2)}) async-start(bf16[32,8,1792]{2,1,0:T(8,128)(2,1)} %bitcast.26), calls=%async_computation | async-start | bytes 1835008 | tf_op jit(solution)/shard_map/all_to_all | solution.py:238
  46.6 23.1 %collective-permute-start.6 = (bf16[192,1536]{1,0:T(8,128)(2,1)}, bf16[192,1536]{1,0:T(8,128)(2,1)}, u32[]{:S(2)}, u32[]{:S(2)}) collective-permute-start(bf16[192,1536]{1,0:T(8,128)(2,1)} %get-tuple-element.33), channel_id=1, source_target_pairs={{0,2},{1,3},{2,4},{3,5},{4,6},{5,7},{6,8},{7,9},{8,10},{9,11},{10,... | collective-permute-start | bytes 1769480 | tf_op jit(solution)/shard_map/ppermute | solution.py:226
  49.6 22.0 %collective-permute-start.8 = (bf16[192,1536]{1,0:T(8,128)(2,1)}, bf16[192,1536]{1,0:T(8,128)(2,1)}, u32[]{:S(2)}, u32[]{:S(2)}) collective-permute-start(bf16[192,1536]{1,0:T(8,128)(2,1)} %get-tuple-element.31), channel_id=1, source_target_pairs={{0,14},{1,15},{2,0},{3,1},{4,2},{5,3},{6,4},{7,5},{8,6},{9,7},{10,... | collective-permute-start | bytes 1769480 | tf_op jit(solution)/shard_map/ppermute | solution.py:226
  61.9 44.8 %collective-permute-start.2 = (bf16[256,1792]{1,0:T(8,128)(2,1)S(1)}, bf16[256,1792]{1,0:T(8,128)(2,1)S(1)}, u32[]{:S(2)}, u32[]{:S(2)}) collective-permute-start(bf16[256,1792]{1,0:T(8,128)(2,1)S(1)} %bitcast.24), channel_id=1, source_target_pairs={{0,1},{1,0},{2,3},{3,2},{4,5},{5,4},{6,7},{7,6},{8,9},{9,8},{10,11... | collective-permute-start | bytes 2752520 | tf_op jit(solution)/shard_map/ppermute | solution.py:242
  63.9 18.2 %collective-permute-start.7 = (bf16[192,1536]{1,0:T(8,128)(2,1)}, bf16[192,1536]{1,0:T(8,128)(2,1)S(1)}, u32[]{:S(2)}, u32[]{:S(2)}) collective-permute-start(bf16[192,1536]{1,0:T(8,128)(2,1)} %get-tuple-element.32), channel_id=1, source_target_pairs={{0,14},{1,15},{2,0},{3,1},{4,2},{5,3},{6,4},{7,5},{8,6},{9,7},{10,... | collective-permute-start | bytes 1769480 | tf_op jit(solution)/shard_map/ppermute | solution.py:226
  67.5 19.5 %collective-permute-start.5 = (bf16[192,1536]{1,0:T(8,128)(2,1)}, bf16[192,1536]{1,0:T(8,128)(2,1)S(1)}, u32[]{:S(2)}, u32[]{:S(2)}) collective-permute-start(bf16[192,1536]{1,0:T(8,128)(2,1)} %get-tuple-element.34), channel_id=1, source_target_pairs={{0,2},{1,3},{2,4},{3,5},{4,6},{5,7},{6,8},{7,9},{8,10},{9,11},{10,... | collective-permute-start | bytes 1769480 | tf_op jit(solution)/shard_map/ppermute | solution.py:226
  69.7 29.9 %collective-permute-start.11 = (bf16[192,1536]{1,0:T(8,128)(2,1)}, bf16[192,1536]{1,0:T(8,128)(2,1)S(1)}, u32[]{:S(2)}, u32[]{:S(2)}) collective-permute-start(bf16[192,1536]{1,0:T(8,128)(2,1)} %collective-permute-done.6.refs_4_), channel_id=1, source_target_pairs={{0,2},{1,3},{2,4},{3,5},{4,6},{5,7},{6,8},{7,9},{8,10},{9,11},{10,... | collective-permute-start | bytes 1769480 | tf_op jit(solution)/shard_map/ppermute | solution.py:226
  71.7 29.9 %collective-permute-start.12 = (bf16[192,1536]{1,0:T(8,128)(2,1)}, bf16[192,1536]{1,0:T(8,128)(2,1)S(1)}, u32[]{:S(2)}, u32[]{:S(2)}) collective-permute-start(bf16[192,1536]{1,0:T(8,128)(2,1)} %collective-permute-done.8.refs_6_), channel_id=1, source_target_pairs={{0,14},{1,15},{2,0},{3,1},{4,2},{5,3},{6,4},{7,5},{8,6},{9,7},{10,... | collective-permute-start | bytes 1769480 | tf_op jit(solution)/shard_map/ppermute | solution.py:226
  82.1 30.6 %collective-permute-start.10 = (bf16[192,1536]{1,0:T(8,128)(2,1)S(1)}, bf16[192,1536]{1,0:T(8,128)(2,1)S(1)}, u32[]{:S(2)}, u32[]{:S(2)}) collective-permute-start(bf16[192,1536]{1,0:T(8,128)(2,1)S(1)} %collective-permute-done.7.refs_5_), channel_id=1, source_target_pairs={{0,14},{1,15},{2,0},{3,1},{4,2},{5,3},{6,4},{7,5},{8,6},{9,7},{10,... | collective-permute-start | bytes 1769480 | tf_op jit(solution)/shard_map/ppermute | solution.py:226
  87.0 25.7 %collective-permute-start.9 = (bf16[192,1536]{1,0:T(8,128)(2,1)S(1)}, bf16[192,1536]{1,0:T(8,128)(2,1)S(1)}, u32[]{:S(2)}, u32[]{:S(2)}) collective-permute-start(bf16[192,1536]{1,0:T(8,128)(2,1)S(1)} %collective-permute-done.5.refs_3_), channel_id=1, source_target_pairs={{0,2},{1,3},{2,4},{3,5},{4,6},{5,7},{6,8},{7,9},{8,10},{9,11},{10,... | collective-permute-start | bytes 1769480 | tf_op jit(solution)/shard_map/ppermute | solution.py:226
  99.6 22.5 %collective-permute-start.14 = (bf16[96,1536]{1,0:T(8,128)(2,1)S(1)}, bf16[96,1536]{1,0:T(8,128)(2,1)S(1)}, u32[]{:S(2)}, u32[]{:S(2)}) collective-permute-start(bf16[96,1536]{1,0:T(8,128)(2,1)S(1)} %slice.52), channel_id=1, source_target_pairs={{0,2},{1,3},{2,4},{3,5},{4,6},{5,7},{6,8},{7,9},{8,10},{9,11},{10,... | collective-permute-start | bytes 884744 | tf_op jit(solution)/shard_map/ppermute | solution.py:226
  101.6 20.5 %collective-permute-start.16 = (bf16[96,1536]{1,0:T(8,128)(2,1)S(1)}, bf16[96,1536]{1,0:T(8,128)(2,1)S(1)}, u32[]{:S(2)}, u32[]{:S(2)}) collective-permute-start(bf16[96,1536]{1,0:T(8,128)(2,1)S(1)} %slice.53), channel_id=1, source_target_pairs={{0,14},{1,15},{2,0},{3,1},{4,2},{5,3},{6,4},{7,5},{8,6},{9,7},{10,... | collective-permute-start | bytes 884744 | tf_op jit(solution)/shard_map/ppermute | solution.py:226
  112.7 11.4 %collective-permute-start.13 = (bf16[96,1536]{1,0:T(8,128)(2,1)S(1)}, bf16[96,1536]{1,0:T(8,128)(2,1)S(1)}, u32[]{:S(2)}, u32[]{:S(2)}) collective-permute-start(bf16[96,1536]{1,0:T(8,128)(2,1)S(1)} %slice.44), channel_id=1, source_target_pairs={{0,2},{1,3},{2,4},{3,5},{4,6},{5,7},{6,8},{7,9},{8,10},{9,11},{10,... | collective-permute-start | bytes 884744 | tf_op jit(solution)/shard_map/ppermute | solution.py:226
  114.7 9.5 %collective-permute-start.15 = (bf16[96,1536]{1,0:T(8,128)(2,1)S(1)}, bf16[96,1536]{1,0:T(8,128)(2,1)S(1)}, u32[]{:S(2)}, u32[]{:S(2)}) collective-permute-start(bf16[96,1536]{1,0:T(8,128)(2,1)S(1)} %slice.46), channel_id=1, source_target_pairs={{0,14},{1,15},{2,0},{3,1},{4,2},{5,3},{6,4},{7,5},{8,6},{9,7},{10,... | collective-permute-start | bytes 884744 | tf_op jit(solution)/shard_map/ppermute | solution.py:226
  126.2 4.3 %collective-permute-start.17 = (bf16[288,1536]{1,0:T(8,128)(2,1)S(1)}, bf16[288,1536]{1,0:T(8,128)(2,1)S(1)}, u32[]{:S(2)}, u32[]{:S(2)}) collective-permute-start(bf16[288,1536]{1,0:T(8,128)(2,1)S(1)} %get-tuple-element.25), channel_id=1, source_target_pairs={{0,1},{1,0},{2,3},{3,2},{4,5},{5,4},{6,7},{7,6},{8,9},{9,8},{10,11... | collective-permute-start | bytes 2654216 | tf_op jit(solution)/shard_map/ppermute | solution.py:263
  131.1 31.1 %copy-start.2 = (f32[128,1536]{1,0:T(8,128)S(1)}, f32[128,1536]{1,0:T(8,128)}, u32[]{:S(2)}) copy-start(f32[128,1536]{1,0:T(8,128)} %copy-done.1) | copy-start | bytes 2359300

commit v3 on v2

--- a/solution.py
+++ b/solution.py
@@ -166,14 +166,14 @@
     accumulate(hidden, second, total_ref, old_ref)
 
 
-def end_kernel(rows_ref, old_ref, *refs):
-    *blocks, mine_ref, other_ref = refs
-    hidden, second = ffn(rows_ref[...], blocks)
+def end_kernel(own_rows, rows_ref, old_ref, *refs):
+    *blocks, out_ref = refs
     half = rows_ref.shape[0] // 2
+    here = slice(0, half) if own_rows else slice(half, 2 * half)
+    hidden, second = ffn(rows_ref[here], blocks)
     for n in range(0, second.shape[1], 512):
-        part = old_ref[:, n : n + 512] + dot(hidden, second[:, n : n + 512])
-        mine_ref[:, n : n + 512] = part[:half]
-        other_ref[:, n : n + 512] = part[half:].astype(bf16)
+        part = old_ref[here, n : n + 512] + dot(hidden, second[:, n : n + 512])
+        out_ref[:, n : n + 512] = part.astype(out_ref.dtype)
 
 
 def pack_kernel(mine_ref, other_ref, packed_ref):
@@ -254,13 +254,19 @@
     (total,) = call(
         more_kernel, (shape(total.shape, f32),), (rows, total, *a3, *b3), flops(2 * units), aliases={1: 0}
     )
-    kept, gone = call(
-        end_kernel,
-        (shape((count, features), f32), shape((count, features), bf16)),
+    (gone,) = call(
+        functools.partial(end_kernel, False),
+        (shape((count, features), bf16),),
         (rows, total, *a4, *b4),
-        flops(units),
+        flops(units) // 2,
     )
     came = lax.ppermute(gone, "dp", sibling)
+    (kept,) = call(
+        functools.partial(end_kernel, True),
+        (shape((count, features), f32),),
+        (rows, total, *a4, *b4),
+        flops(units) // 2,
+    )
     (packed,) = call(pack_kernel, (shape(sent.shape, bf16),), (kept, came), 10_000_000)
     back = exchange(packed)
     (out,) = call(combine_kernel, (shape((tok, features), bf16),), (back, residual, *weights), 10_000_000)

time: 164 us -> 164 us (level)
    pallas_call x6 -> x7, Pallas kernels: 15.1 us -> 15.4 us  [call(): pl.pallas_call(kernel, out_shape=outs, in_specs=[pl.BlockSpec(memory_spac...]
  transfers between devices with their start and end apart: 19 -> 19, of which waited for: 6 -> 6; matrix products, arithmetic and copies ran while one was open for 3% -> 3% of each run, Pallas kernels for 7% -> 8%
where the time goes in v3:
time: 164 us; the launch traced here: 163 us
  starting transfers between devices  73.3 us (45%)
  waiting for transfers between devices  34.7 us (21%)
  blocking collectives  31.1 us (19%)
  Pallas kernels  15.4 us (9%)
  local copies, waits for them, and re-layouts  7.83 us (5%)
    all_to_all x1, blocking collectives, exchange(): lax.all_to_all(parts, 'expert', split_axis=0, concat_axis=0, tiled=True)  31.1 us
    ppermute x6, starting transfers between devices, step(): lax.ppermute(b, 'dp', down)  29 us
    pallas_call x7, Pallas kernels, call(): pl.pallas_call(kernel, out_shape=outs, in_specs=[pl.BlockSpec(memory_spac...  15.4 us
    ppermute x2, starting transfers between devices, shards(): a1, b1 = (lax.ppermute(own, 'dp', up), lax.ppermute(own, 'dp', down))  15.4 us
    ppermute x6, waiting for transfers between devices, step(): lax.ppermute(a, 'dp', up)  12.8 us
    ppermute x6, starting transfers between devices, step(): lax.ppermute(a, 'dp', up)  11.8 us
    all_to_all x1, starting transfers between devices, exchange(): lax.all_to_all(parts, 'expert', split_axis=0, concat_axis=0, tiled=True)  10.2 us
    ppermute x2, waiting for transfers between devices, shards(): a1, b1 = (lax.ppermute(own, 'dp', up), lax.ppermute(own, 'dp', down))  8.09 us
  transfers between devices with their start and end apart: 19, of which 6 were waited for; matrix products, arithmetic and copies ran while one was open for 3% of the time, Pallas kernels for 8%

profile of v3, /device:TPU:8, one launch (start us, length us, event | category | flops | bytes accessed | tf_op | source)
XLA Modules:
  0.0 162.7 jit_solution(1513046113392105447)
XLA Ops:
  0.9 1.7 %collective-permute-start = (bf16[16,1536]{1,0:T(8,128)(2,1)S(1)}, bf16[16,1536]{1,0:T(8,128)(2,1)S(1)}, u32[]{:S(2)}, u32[]{:S(2)}) collective-permute-start(bf16[16,1536]{1,0:T(8,128)(2,1)S(1)} %get-tuple-element.32), channel_id=1, source_target_pairs={{0,1},{1,2},{2,3},{3,4},{4,5},{5,6},{6,7},{7,8},{8,9},{9,10},{10,1... | collective-permute-start | bytes 147464 | tf_op jit(solution)/shard_map/ppermute | solution.py:218
  2.7 1.4 collective-permute-start.1
  4.1 1.9 %constant_dynamic-update-slice_fusion.1 = bf16[2,192,1536]{2,1,0:T(8,128)(2,1)} fusion(bf16[1,192,1536]{2,1,0:T(8,128)(2,1)} %param.11), kind=kLoop, calls=%fused_computation.7 | loop fusion | bytes 1179648
  6.9 6.8 %collective-permute-start.3 = (bf16[2,192,1536]{2,1,0:T(8,128)(2,1)}, bf16[2,192,1536]{2,1,0:T(8,128)(2,1)S(1)}, u32[]{:S(2)}, u32[]{:S(2)}) collective-permute-start(bf16[2,192,1536]{2,1,0:T(8,128)(2,1)} %constant_dynamic-update-slice_fusion.refs_0_), channel_id=1, source_target_pairs={{0,2},{1,3},{2,4},{3,5},{4,6},{5,7},{6,8},{7,9},{8,10},{9,11},{10,... | collective-permute-start | bytes 3538952 | tf_op jit(solution)/shard_map/ppermute | solution.py:223
  13.7 8.6 %collective-permute-start.4 = (bf16[2,192,1536]{2,1,0:T(8,128)(2,1)}, bf16[2,192,1536]{2,1,0:T(8,128)(2,1)S(1)}, u32[]{:S(2)}, u32[]{:S(2)}) collective-permute-start(bf16[2,192,1536]{2,1,0:T(8,128)(2,1)} %constant_dynamic-update-slice_fusion.refs_0_), channel_id=1, source_target_pairs={{0,14},{1,15},{2,0},{3,1},{4,2},{5,3},{6,4},{7,5},{8,6},{9,7},{10,... | collective-permute-start | bytes 3538952 | tf_op jit(solution)/shard_map/ppermute | solution.py:223
  22.4 3.0 %shard_map.73 = (bf16[256,1792]{1,0:T(8,128)(2,1)S(1)}, f32[128,1536]{1,0:T(8,128)S(1)}, bf16[128,256]{1,0:T(8,128)(2,1)S(1)}, bf16[128,256]{1,0:T(8,128)(2,1)S(...) custom-call(bf16[128,1536]{1,0:T(8,128)(2,1)S(1)} %bitcast.27, ...), custom_call_target="tpu_custom_call" | custom-call | flops 20000000000 | bytes 2655232 | tf_op jit(solution)/shard_map/pallas_call | solution.py:28
  27.2 10.2 %all-to-all-start = ((bf16[32,8,1792]{2,1,0:T(8,128)(2,1)}), bf16[32,8,1792]{2,1,0:T(8,128)(2,1)S(1)}, u32[]{:S(2)}, u32[]{:S(2)}) async-start(bf16[32,8,1792]{2,1,0:T(8,128)(2,1)} %bitcast.26), calls=%async_computation | async-start | bytes 1835008 | tf_op jit(solution)/shard_map/all_to_all | solution.py:238
  37.4 8.1 %collective-permute-done.3.refs_1_ = bf16[2,192,1536]{2,1,0:T(8,128)(2,1)S(1)} collective-permute-done((bf16[2,192,1536]{2,1,0:T(8,128)(2,1)}, bf16[2,192,1536]{2,1,0:T(8,128)(2,1)S(1)}, u32[]{:S(2)}, u32[]{:S(2)}) %collective-permute-start.3) | collective-permute-done | bytes 1179680 | tf_op jit(solution)/shard_map/ppermute | solution.py:223
  46.6 1.9 %collective-permute-start.6 = (bf16[192,1536]{1,0:T(8,128)(2,1)}, bf16[192,1536]{1,0:T(8,128)(2,1)}, u32[]{:S(2)}, u32[]{:S(2)}) collective-permute-start(bf16[192,1536]{1,0:T(8,128)(2,1)} %get-tuple-element.29), channel_id=1, source_target_pairs={{0,2},{1,3},{2,4},{3,5},{4,6},{5,7},{6,8},{7,9},{8,10},{9,11},{10,... | collective-permute-start | bytes 1769480 | tf_op jit(solution)/shard_map/ppermute | solution.py:226
  49.6 5.1 %collective-permute-start.8 = (bf16[192,1536]{1,0:T(8,128)(2,1)}, bf16[192,1536]{1,0:T(8,128)(2,1)}, u32[]{:S(2)}, u32[]{:S(2)}) collective-permute-start(bf16[192,1536]{1,0:T(8,128)(2,1)} %get-tuple-element.27), channel_id=1, source_target_pairs={{0,14},{1,15},{2,0},{3,1},{4,2},{5,3},{6,4},{7,5},{8,6},{9,7},{10,... | collective-permute-start | bytes 1769480 | tf_op jit(solution)/shard_map/ppermute | solution.py:226
  54.8 7.2 %all-to-all-done = bf16[32,8,1792]{2,1,0:T(8,128)(2,1)S(1)} async-done(((bf16[32,8,1792]{2,1,0:T(8,128)(2,1)}), bf16[32,8,1792]{2,1,0:T(8,128)(2,1)S(1)}, u32[]{:S(2)}, u32[]{:S(2)}) %all-to-all-start) | async-done | bytes 917536 | tf_op jit(solution)/shard_map/all_to_all | solution.py:238
  61.9 1.9 %collective-permute-start.2 = (bf16[256,1792]{1,0:T(8,128)(2,1)S(1)}, bf16[256,1792]{1,0:T(8,128)(2,1)S(1)}, u32[]{:S(2)}, u32[]{:S(2)}) collective-permute-start(bf16[256,1792]{1,0:T(8,128)(2,1)S(1)} %bitcast.24), channel_id=1, source_target_pairs={{0,1},{1,0},{2,3},{3,2},{4,5},{5,4},{6,7},{7,6},{8,9},{9,8},{10,11... | collective-permute-start | bytes 2752520 | tf_op jit(solution)/shard_map/ppermute | solution.py:242
  63.8 3.6 %collective-permute-start.7 = (bf16[192,1536]{1,0:T(8,128)(2,1)}, bf16[192,1536]{1,0:T(8,128)(2,1)S(1)}, u32[]{:S(2)}, u32[]{:S(2)}) collective-permute-start(bf16[192,1536]{1,0:T(8,128)(2,1)} %get-tuple-element.28), channel_id=1, source_target_pairs={{0,14},{1,15},{2,0},{3,1},{4,2},{5,3},{6,4},{7,5},{8,6},{9,7},{10,... | collective-permute-start | bytes 1769480 | tf_op jit(solution)/shard_map/ppermute | solution.py:226
  67.5 2.2 %collective-permute-start.5 = (bf16[192,1536]{1,0:T(8,128)(2,1)}, bf16[192,1536]{1,0:T(8,128)(2,1)S(1)}, u32[]{:S(2)}, u32[]{:S(2)}) collective-permute-start(bf16[192,1536]{1,0:T(8,128)(2,1)} %get-tuple-element.30), channel_id=1, source_target_pairs={{0,2},{1,3},{2,4},{3,5},{4,6},{5,7},{6,8},{7,9},{8,10},{9,11},{10,... | collective-permute-start | bytes 1769480 | tf_op jit(solution)/shard_map/ppermute | solution.py:226
  69.7 1.9 %collective-permute-start.11 = (bf16[192,1536]{1,0:T(8,128)(2,1)}, bf16[192,1536]{1,0:T(8,128)(2,1)S(1)}, u32[]{:S(2)}, u32[]{:S(2)}) collective-permute-start(bf16[192,1536]{1,0:T(8,128)(2,1)} %collective-permute-done.6.refs_4_), channel_id=1, source_target_pairs={{0,2},{1,3},{2,4},{3,5},{4,6},{5,7},{6,8},{7,9},{8,10},{9,11},{10,... | collective-permute-start | bytes 1769480 | tf_op jit(solution)/shard_map/ppermute | solution.py:226
  71.7 5.1 %collective-permute-start.12 = (bf16[192,1536]{1,0:T(8,128)(2,1)}, bf16[192,1536]{1,0:T(8,128)(2,1)S(1)}, u32[]{:S(2)}, u32[]{:S(2)}) collective-permute-start(bf16[192,1536]{1,0:T(8,128)(2,1)} %collective-permute-done.8.refs_6_), channel_id=1, source_target_pairs={{0,14},{1,15},{2,0},{3,1},{4,2},{5,3},{6,4},{7,5},{8,6},{9,7},{10,... | collective-permute-start | bytes 1769480 | tf_op jit(solution)/shard_map/ppermute | solution.py:226
  76.8 5.3 %collective-permute-done.7.refs_5_ = bf16[192,1536]{1,0:T(8,128)(2,1)S(1)} collective-permute-done((bf16[192,1536]{1,0:T(8,128)(2,1)}, bf16[192,1536]{1,0:T(8,128)(2,1)S(1)}, u32[]{:S(2)}, u32[]{:S(2)}) %collective-permute-start.7) | collective-permute-done | bytes 589856 | tf_op jit(solution)/shard_map/ppermute | solution.py:226
  82.1 4.8 %collective-permute-start.10 = (bf16[192,1536]{1,0:T(8,128)(2,1)S(1)}, bf16[192,1536]{1,0:T(8,128)(2,1)S(1)}, u32[]{:S(2)}, u32[]{:S(2)}) collective-permute-start(bf16[192,1536]{1,0:T(8,128)(2,1)S(1)} %collective-permute-done.7.refs_5_), channel_id=1, source_target_pairs={{0,14},{1,15},{2,0},{3,1},{4,2},{5,3},{6,4},{7,5},{8,6},{9,7},{10,... | collective-permute-start | bytes 1769480 | tf_op jit(solution)/shard_map/ppermute | solution.py:226
  87.0 1.9 %collective-permute-start.9 = (bf16[192,1536]{1,0:T(8,128)(2,1)S(1)}, bf16[192,1536]{1,0:T(8,128)(2,1)S(1)}, u32[]{:S(2)}, u32[]{:S(2)}) collective-permute-start(bf16[192,1536]{1,0:T(8,128)(2,1)S(1)} %collective-permute-done.5.refs_3_), channel_id=1, source_target_pairs={{0,2},{1,3},{2,4},{3,5},{4,6},{5,7},{6,8},{7,9},{8,10},{9,11},{10,... | collective-permute-start | bytes 1769480 | tf_op jit(solution)/shard_map/ppermute | solution.py:226
  88.9 10.7 %collective-permute-done.11.refs_1_ = bf16[192,1536]{1,0:T(8,128)(2,1)S(1)} collective-permute-done((bf16[192,1536]{1,0:T(8,128)(2,1)}, bf16[192,1536]{1,0:T(8,128)(2,1)S(1)}, u32[]{:S(2)}, u32[]{:S(2)}) %collective-permute-start.11) | collective-permute-done | bytes 589856 | tf_op jit(solution)/shard_map/ppermute | solution.py:226
  99.6 1.9 %collective-permute-start.14 = (bf16[96,1536]{1,0:T(8,128)(2,1)S(1)}, bf16[96,1536]{1,0:T(8,128)(2,1)S(1)}, u32[]{:S(2)}, u32[]{:S(2)}) collective-permute-start(bf16[96,1536]{1,0:T(8,128)(2,1)S(1)} %slice.52), channel_id=1, source_target_pairs={{0,2},{1,3},{2,4},{3,5},{4,6},{5,7},{6,8},{7,9},{8,10},{9,11},{10,... | collective-permute-start | bytes 884744 | tf_op jit(solution)/shard_map/ppermute | solution.py:226
  101.6 5.1 %collective-permute-start.16 = (bf16[96,1536]{1,0:T(8,128)(2,1)S(1)}, bf16[96,1536]{1,0:T(8,128)(2,1)S(1)}, u32[]{:S(2)}, u32[]{:S(2)}) collective-permute-start(bf16[96,1536]{1,0:T(8,128)(2,1)S(1)} %slice.53), channel_id=1, source_target_pairs={{0,14},{1,15},{2,0},{3,1},{4,2},{5,3},{6,4},{7,5},{8,6},{9,7},{10,... | collective-permute-start | bytes 884744 | tf_op jit(solution)/shard_map/ppermute | solution.py:226
  106.8 5.9 %shard_map.74 = (bf16[576,1536]{1,0:T(8,128)(2,1)S(1)}, f32[576,1536]{1,0:T(8,128)S(1)}) custom-call(bf16[256,1792]{1,0:T(8,128)(2,1)S(1)} %bitcast.25, bf16[256,1792]{1,0:T(8,128)(2,1)S(1)} %collective-permute-done.2.other_ref, bf16[2,192,1536]{2,1,0:T(8,128)(2,1)} %constant_dynamic-update-slice_fusion.refs_0_, ...), custom_call_target="tpu_custom_call" | custom-call | flops 3397386240 | bytes 13041664 | tf_op jit(solution)/shard_map/pallas_call | solution.py:28
  112.7 1.9 %collective-permute-start.13 = (bf16[96,1536]{1,0:T(8,128)(2,1)S(1)}, bf16[96,1536]{1,0:T(8,128)(2,1)S(1)}, u32[]{:S(2)}, u32[]{:S(2)}) collective-permute-start(bf16[96,1536]{1,0:T(8,128)(2,1)S(1)} %slice.44), channel_id=1, source_target_pairs={{0,2},{1,3},{2,4},{3,5},{4,6},{5,7},{6,8},{7,9},{8,10},{9,11},{10,... | collective-permute-start | bytes 884744 | tf_op jit(solution)/shard_map/ppermute | solution.py:226
  114.7 5.1 %collective-permute-start.15 = (bf16[96,1536]{1,0:T(8,128)(2,1)S(1)}, bf16[96,1536]{1,0:T(8,128)(2,1)S(1)}, u32[]{:S(2)}, u32[]{:S(2)}) collective-permute-start(bf16[96,1536]{1,0:T(8,128)(2,1)S(1)} %slice.46), channel_id=1, source_target_pairs={{0,14},{1,15},{2,0},{3,1},{4,2},{5,3},{6,4},{7,5},{8,6},{9,7},{10,... | collective-permute-start | bytes 884744 | tf_op jit(solution)/shard_map/ppermute | solution.py:226
  119.8 2.3 %shard_map.75.old_ref = f32[576,1536]{1,0:T(8,128)S(1)} custom-call(bf16[576,1536]{1,0:T(8,128)(2,1)S(1)} %get-tuple-element.17.rows_ref, f32[576,1536]{1,0:T(8,128)S(1)} %get-tuple-element.19.old_ref, bf16[192,1536]{1,0:T(8,128)(2,1)S(1)} %collective-permute-done.9.refs_0_, ...), custom_call_target="tpu_custom_call", output_to_operand_aliasing={{}: (1, {})} | custom-call | flops 1358954496 | bytes 11206656 | tf_op jit(solution)/shard_map/pallas_call | solution.py:28
  122.1 2.1 %collective-permute-done.13.refs_0_ = bf16[96,1536]{1,0:T(8,128)(2,1)S(1)} collective-permute-done((bf16[96,1536]{1,0:T(8,128)(2,1)S(1)}, bf16[96,1536]{1,0:T(8,128)(2,1)S(1)}, u32[]{:S(2)}, u32[]{:S(2)}) %collective-permute-start.13) | collective-permute-done | bytes 294944 | tf_op jit(solution)/shard_map/ppermute | solution.py:226
  125.3 1.9 %collective-permute-start.17 = (bf16[288,1536]{1,0:T(8,128)(2,1)S(1)}, bf16[288,1536]{1,0:T(8,128)(2,1)S(1)}, u32[]{:S(2)}, u32[]{:S(2)}) collective-permute-start(bf16[288,1536]{1,0:T(8,128)(2,1)S(1)} %shard_map.77), channel_id=1, source_target_pairs={{0,1},{1,0},{2,3},{3,2},{4,5},{5,4},{6,7},{7,6},{8,9},{9,8},{10,11... | collective-permute-start | bytes 2654216 | tf_op jit(solution)/shard_map/ppermute | solution.py:263
  127.3 1.1 shard_map.76.mine_ref
  128.4 1.2 collective-permute-done.17.other_ref
  130.3 31.1 %all_to_all.10 = bf16[32,8,1792]{2,1,0:T(8,128)(2,1)S(1)} all-to-all(bf16[32,8,1792]{2,1,0:T(8,128)(2,1)S(1)} %bitcast.22), channel_id=1, replica_groups=mesh['expert'=32,'dp'=16] {'expert'}, dimensions={0} | all-to-all | bytes 1835008 | tf_op jit(solution)/shard_map/all_to_all | solution.py:238
  161.4 1.3 shard_map.79
  (42 shorter events, 7.7 us)
Async XLA Ops:
  0.0 6.0 %copy-start.7 = (bf16[1,192,1536]{2,1,0:T(8,128)(2,1)S(1)}, bf16[1,192,1536]{2,1,0:T(8,128)(2,1)}, u32[]{:S(2)}) copy-start(bf16[1,192,1536]{2,1,0:T(8,128)(2,1)} %param.12) | copy-start | bytes 1769476
  0.9 21.5 %collective-permute-start = (bf16[16,1536]{1,0:T(8,128)(2,1)S(1)}, bf16[16,1536]{1,0:T(8,128)(2,1)S(1)}, u32[]{:S(2)}, u32[]{:S(2)}) collective-permute-start(bf16[16,1536]{1,0:T(8,128)(2,1)S(1)} %get-tuple-element.32), channel_id=1, source_target_pairs={{0,1},{1,2},{2,3},{3,4},{4,5},{5,6},{6,7},{7,8},{8,9},{9,10},{10,1... | collective-permute-start | bytes 147464 | tf_op jit(solution)/shard_map/ppermute | solution.py:218
  2.6 19.7 %copy-start.8 = (bf16[1536]{0:T(1024)(128)(2,1)S(1)}, bf16[1536]{0:T(1024)(128)(2,1)}, u32[]{:S(2)}) copy-start(bf16[1536]{0:T(1024)(128)(2,1)} %param.9) | copy-start | bytes 9220
  2.6 19.7 %copy-start.3 = (bf16[1,128,1536]{2,1,0:T(8,128)(2,1)S(1)}, bf16[1,128,1536]{2,1,0:T(8,128)(2,1)}, u32[]{:S(2)}) copy-start(bf16[1,128,1536]{2,1,0:T(8,128)(2,1)} %param.7) | copy-start | bytes 1179652
  2.7 19.7 %copy-start.4 = (bf16[31,1536]{1,0:T(8,128)(2,1)S(1)}, bf16[31,1536]{1,0:T(8,128)(2,1)}, u32[]{:S(2)}) copy-start(bf16[31,1536]{1,0:T(8,128)(2,1)} %kernel_ref.1) | copy-start | bytes 285700
  2.7 19.7 %copy-start.5 = (bf16[1536,32]{0,1:T(8,128)(2,1)S(1)}, bf16[1536,32]{0,1:T(8,128)(2,1)}, u32[]{:S(2)}) copy-start(bf16[1536,32]{0,1:T(8,128)(2,1)} %param.10) | copy-start | bytes 294916
  2.7 19.7 %copy-start.6 = (s32[1,128,2]{1,2,0:T(2,128)S(1)}, s32[1,128,2]{1,2,0:T(2,128)}, u32[]{:S(2)}) copy-start(s32[1,128,2]{1,2,0:T(2,128)} %param.13) | copy-start | bytes 3076
  2.7 19.7 %collective-permute-start.1 = (bf16[16,1536]{1,0:T(8,128)(2,1)S(1)}, bf16[16,1536]{1,0:T(8,128)(2,1)S(1)}, u32[]{:S(2)}, u32[]{:S(2)}) collective-permute-start(bf16[16,1536]{1,0:T(8,128)(2,1)S(1)} %get-tuple-element.31), channel_id=1, source_target_pairs={{1,0},{2,1},{3,2},{4,3},{5,4},{6,5},{7,6},{8,7},{9,8},{10,9},{11,1... | collective-permute-start | bytes 147464 | tf_op jit(solution)/shard_map/ppermute | solution.py:219
  6.9 38.6 %collective-permute-start.3 = (bf16[2,192,1536]{2,1,0:T(8,128)(2,1)}, bf16[2,192,1536]{2,1,0:T(8,128)(2,1)S(1)}, u32[]{:S(2)}, u32[]{:S(2)}) collective-permute-start(bf16[2,192,1536]{2,1,0:T(8,128)(2,1)} %constant_dynamic-update-slice_fusion.refs_0_), channel_id=1, source_target_pairs={{0,2},{1,3},{2,4},{3,5},{4,6},{5,7},{6,8},{7,9},{8,10},{9,11},{10,... | collective-permute-start | bytes 3538952 | tf_op jit(solution)/shard_map/ppermute | solution.py:223
  13.7 34.8 %collective-permute-start.4 = (bf16[2,192,1536]{2,1,0:T(8,128)(2,1)}, bf16[2,192,1536]{2,1,0:T(8,128)(2,1)S(1)}, u32[]{:S(2)}, u32[]{:S(2)}) collective-permute-start(bf16[2,192,1536]{2,1,0:T(8,128)(2,1)} %constant_dynamic-update-slice_fusion.refs_0_), channel_id=1, source_target_pairs={{0,14},{1,15},{2,0},{3,1},{4,2},{5,3},{6,4},{7,5},{8,6},{9,7},{10,... | collective-permute-start | bytes 3538952 | tf_op jit(solution)/shard_map/ppermute | solution.py:223
  25.4 0.9 copy-start
  26.4 0.9 copy-start.1
  27.2 34.7 %all-to-all-start = ((bf16[32,8,1792]{2,1,0:T(8,128)(2,1)}), bf16[32,8,1792]{2,1,0:T(8,128)(2,1)S(1)}, u32[]{:S(2)}, u32[]{:S(2)}) async-start(bf16[32,8,1792]{2,1,0:T(8,128)(2,1)} %bitcast.26), calls=%async_computation | async-start | bytes 1835008 | tf_op jit(solution)/shard_map/all_to_all | solution.py:238
  46.6 23.1 %collective-permute-start.6 = (bf16[192,1536]{1,0:T(8,128)(2,1)}, bf16[192,1536]{1,0:T(8,128)(2,1)}, u32[]{:S(2)}, u32[]{:S(2)}) collective-permute-start(bf16[192,1536]{1,0:T(8,128)(2,1)} %get-tuple-element.29), channel_id=1, source_target_pairs={{0,2},{1,3},{2,4},{3,5},{4,6},{5,7},{6,8},{7,9},{8,10},{9,11},{10,... | collective-permute-start | bytes 1769480 | tf_op jit(solution)/shard_map/ppermute | solution.py:226
  49.6 22.0 %collective-permute-start.8 = (bf16[192,1536]{1,0:T(8,128)(2,1)}, bf16[192,1536]{1,0:T(8,128)(2,1)}, u32[]{:S(2)}, u32[]{:S(2)}) collective-permute-start(bf16[192,1536]{1,0:T(8,128)(2,1)} %get-tuple-element.27), channel_id=1, source_target_pairs={{0,14},{1,15},{2,0},{3,1},{4,2},{5,3},{6,4},{7,5},{8,6},{9,7},{10,... | collective-permute-start | bytes 1769480 | tf_op jit(solution)/shard_map/ppermute | solution.py:226
  61.9 44.8 %collective-permute-start.2 = (bf16[256,1792]{1,0:T(8,128)(2,1)S(1)}, bf16[256,1792]{1,0:T(8,128)(2,1)S(1)}, u32[]{:S(2)}, u32[]{:S(2)}) collective-permute-start(bf16[256,1792]{1,0:T(8,128)(2,1)S(1)} %bitcast.24), channel_id=1, source_target_pairs={{0,1},{1,0},{2,3},{3,2},{4,5},{5,4},{6,7},{7,6},{8,9},{9,8},{10,11... | collective-permute-start | bytes 2752520 | tf_op jit(solution)/shard_map/ppermute | solution.py:242
  63.8 18.2 %collective-permute-start.7 = (bf16[192,1536]{1,0:T(8,128)(2,1)}, bf16[192,1536]{1,0:T(8,128)(2,1)S(1)}, u32[]{:S(2)}, u32[]{:S(2)}) collective-permute-start(bf16[192,1536]{1,0:T(8,128)(2,1)} %get-tuple-element.28), channel_id=1, source_target_pairs={{0,14},{1,15},{2,0},{3,1},{4,2},{5,3},{6,4},{7,5},{8,6},{9,7},{10,... | collective-permute-start | bytes 1769480 | tf_op jit(solution)/shard_map/ppermute | solution.py:226
  67.5 19.5 %collective-permute-start.5 = (bf16[192,1536]{1,0:T(8,128)(2,1)}, bf16[192,1536]{1,0:T(8,128)(2,1)S(1)}, u32[]{:S(2)}, u32[]{:S(2)}) collective-permute-start(bf16[192,1536]{1,0:T(8,128)(2,1)} %get-tuple-element.30), channel_id=1, source_target_pairs={{0,2},{1,3},{2,4},{3,5},{4,6},{5,7},{6,8},{7,9},{8,10},{9,11},{10,... | collective-permute-start | bytes 1769480 | tf_op jit(solution)/shard_map/ppermute | solution.py:226
  69.7 29.9 %collective-permute-start.11 = (bf16[192,1536]{1,0:T(8,128)(2,1)}, bf16[192,1536]{1,0:T(8,128)(2,1)S(1)}, u32[]{:S(2)}, u32[]{:S(2)}) collective-permute-start(bf16[192,1536]{1,0:T(8,128)(2,1)} %collective-permute-done.6.refs_4_), channel_id=1, source_target_pairs={{0,2},{1,3},{2,4},{3,5},{4,6},{5,7},{6,8},{7,9},{8,10},{9,11},{10,... | collective-permute-start | bytes 1769480 | tf_op jit(solution)/shard_map/ppermute | solution.py:226
  71.7 29.9 %collective-permute-start.12 = (bf16[192,1536]{1,0:T(8,128)(2,1)}, bf16[192,1536]{1,0:T(8,128)(2,1)S(1)}, u32[]{:S(2)}, u32[]{:S(2)}) collective-permute-start(bf16[192,1536]{1,0:T(8,128)(2,1)} %collective-permute-done.8.refs_6_), channel_id=1, source_target_pairs={{0,14},{1,15},{2,0},{3,1},{4,2},{5,3},{6,4},{7,5},{8,6},{9,7},{10,... | collective-permute-start | bytes 1769480 | tf_op jit(solution)/shard_map/ppermute | solution.py:226
  82.1 30.6 %collective-permute-start.10 = (bf16[192,1536]{1,0:T(8,128)(2,1)S(1)}, bf16[192,1536]{1,0:T(8,128)(2,1)S(1)}, u32[]{:S(2)}, u32[]{:S(2)}) collective-permute-start(bf16[192,1536]{1,0:T(8,128)(2,1)S(1)} %collective-permute-done.7.refs_5_), channel_id=1, source_target_pairs={{0,14},{1,15},{2,0},{3,1},{4,2},{5,3},{6,4},{7,5},{8,6},{9,7},{10,... | collective-permute-start | bytes 1769480 | tf_op jit(solution)/shard_map/ppermute | solution.py:226
  87.0 25.7 %collective-permute-start.9 = (bf16[192,1536]{1,0:T(8,128)(2,1)S(1)}, bf16[192,1536]{1,0:T(8,128)(2,1)S(1)}, u32[]{:S(2)}, u32[]{:S(2)}) collective-permute-start(bf16[192,1536]{1,0:T(8,128)(2,1)S(1)} %collective-permute-done.5.refs_3_), channel_id=1, source_target_pairs={{0,2},{1,3},{2,4},{3,5},{4,6},{5,7},{6,8},{7,9},{8,10},{9,11},{10,... | collective-permute-start | bytes 1769480 | tf_op jit(solution)/shard_map/ppermute | solution.py:226
  99.6 22.5 %collective-permute-start.14 = (bf16[96,1536]{1,0:T(8,128)(2,1)S(1)}, bf16[96,1536]{1,0:T(8,128)(2,1)S(1)}, u32[]{:S(2)}, u32[]{:S(2)}) collective-permute-start(bf16[96,1536]{1,0:T(8,128)(2,1)S(1)} %slice.52), channel_id=1, source_target_pairs={{0,2},{1,3},{2,4},{3,5},{4,6},{5,7},{6,8},{7,9},{8,10},{9,11},{10,... | collective-permute-start | bytes 884744 | tf_op jit(solution)/shard_map/ppermute | solution.py:226
  101.6 20.5 %collective-permute-start.16 = (bf16[96,1536]{1,0:T(8,128)(2,1)S(1)}, bf16[96,1536]{1,0:T(8,128)(2,1)S(1)}, u32[]{:S(2)}, u32[]{:S(2)}) collective-permute-start(bf16[96,1536]{1,0:T(8,128)(2,1)S(1)} %slice.53), channel_id=1, source_target_pairs={{0,14},{1,15},{2,0},{3,1},{4,2},{5,3},{6,4},{7,5},{8,6},{9,7},{10,... | collective-permute-start | bytes 884744 | tf_op jit(solution)/shard_map/ppermute | solution.py:226
  112.7 11.4 %collective-permute-start.13 = (bf16[96,1536]{1,0:T(8,128)(2,1)S(1)}, bf16[96,1536]{1,0:T(8,128)(2,1)S(1)}, u32[]{:S(2)}, u32[]{:S(2)}) collective-permute-start(bf16[96,1536]{1,0:T(8,128)(2,1)S(1)} %slice.44), channel_id=1, source_target_pairs={{0,2},{1,3},{2,4},{3,5},{4,6},{5,7},{6,8},{7,9},{8,10},{9,11},{10,... | collective-permute-start | bytes 884744 | tf_op jit(solution)/shard_map/ppermute | solution.py:226
  114.7 9.5 %collective-permute-start.15 = (bf16[96,1536]{1,0:T(8,128)(2,1)S(1)}, bf16[96,1536]{1,0:T(8,128)(2,1)S(1)}, u32[]{:S(2)}, u32[]{:S(2)}) collective-permute-start(bf16[96,1536]{1,0:T(8,128)(2,1)S(1)} %slice.46), channel_id=1, source_target_pairs={{0,14},{1,15},{2,0},{3,1},{4,2},{5,3},{6,4},{7,5},{8,6},{9,7},{10,... | collective-permute-start | bytes 884744 | tf_op jit(solution)/shard_map/ppermute | solution.py:226
  125.3 4.3 %collective-permute-start.17 = (bf16[288,1536]{1,0:T(8,128)(2,1)S(1)}, bf16[288,1536]{1,0:T(8,128)(2,1)S(1)}, u32[]{:S(2)}, u32[]{:S(2)}) collective-permute-start(bf16[288,1536]{1,0:T(8,128)(2,1)S(1)} %shard_map.77), channel_id=1, source_target_pairs={{0,1},{1,0},{2,3},{3,2},{4,5},{5,4},{6,7},{7,6},{8,9},{9,8},{10,11... | collective-permute-start | bytes 2654216 | tf_op jit(solution)/shard_map/ppermute | solution.py:263
  130.3 31.1 %copy-start.2 = (f32[128,1536]{1,0:T(8,128)S(1)}, f32[128,1536]{1,0:T(8,128)}, u32[]{:S(2)}) copy-start(f32[128,1536]{1,0:T(8,128)} %copy-done.1) | copy-start | bytes 2359300

commit v4 on v3

--- a/solution.py
+++ b/solution.py
@@ -39,6 +39,17 @@
 
 def shape(dims, dtype):
     return jax.ShapeDtypeStruct(dims, dtype)
+
+
+def join_kernel(first_ref, second_ref, out_ref, sems):
+    copies = [
+        pltpu.make_async_copy(ref.at[0], out_ref.at[k], sems.at[k])
+        for k, ref in enumerate((first_ref, second_ref))
+    ]
+    for copy in copies:
+        copy.start()
+    for copy in copies:
+        copy.wait()
 
 
 def front_kernel(taps, x_ref, low_ref, high_ref, kernel_ref, gain_ref, router_ref, routes_ref,
@@ -219,7 +230,13 @@
     high = lax.ppermute(frames[:HALO], "dp", [(i + 1, i) for i in range(dp - 1)])
 
     units = w_in.shape[1]
-    own = jnp.concatenate([w_in, w_out], axis=0)
+    own = pl.pallas_call(
+        join_kernel,
+        out_shape=shape((2, *w_in.shape[1:]), bf16),
+        in_specs=[pl.BlockSpec(memory_space=pl.ANY)] * 2,
+        out_specs=pl.BlockSpec(memory_space=pltpu.VMEM),
+        scratch_shapes=[pltpu.SemaphoreType.DMA((2,))],
+    )(w_in, w_out)
     a1, b1 = lax.ppermute(own, "dp", up), lax.ppermute(own, "dp", down)
 
     def step(ups, downs):

time: 164 us -> 166 us (1.012)
  Pallas kernels: 15.4 us -> 18.6 us
    ppermute x2, waiting for transfers between devices: 8.09 us -> 5.51 us  [shards(): a1, b1 = (lax.ppermute(own, 'dp', up), lax.ppermute(own, 'dp', down))]
    all_to_all x1, waiting for transfers between devices: 7.16 us -> 9.67 us  [exchange(): lax.all_to_all(parts, 'expert', split_axis=0, concat_axis=0, tiled=True)]
    pallas_call x0 -> x1, Pallas kernels: none -> 2.3 us  [shards(): pl.pallas_call(join_kernel, out_shape=shape((2, *w_in.shape[1:]), bf16),...]
    unnamed x19 -> x32, local copies, waits for them, and re-layouts: 3.76 us -> 3.45 us
  transfers between devices with their start and end apart: 19 -> 19, of which waited for: 6 -> 6; matrix products, arithmetic and copies ran while one was open for 3% -> 1% of each run, Pallas kernels for 8% -> 9%
where the time goes in v4:
time: 166 us; the launch traced here: 165 us
  starting transfers between devices  73.5 us (44%)
  waiting for transfers between devices  34.7 us (21%)
  blocking collectives  31.1 us (19%)
  Pallas kernels  18.6 us (11%)
  local copies, waits for them, and re-layouts  6.57 us (4%)
    all_to_all x1, blocking collectives, exchange(): lax.all_to_all(parts, 'expert', split_axis=0, concat_axis=0, tiled=True)  31.1 us
    ppermute x6, starting transfers between devices, step(): lax.ppermute(b, 'dp', down)  29.2 us
    pallas_call x7, Pallas kernels, call(): pl.pallas_call(kernel, out_shape=outs, in_specs=[pl.BlockSpec(memory_spac...  16.3 us
    ppermute x2, starting transfers between devices, shards(): a1, b1 = (lax.ppermute(own, 'dp', up), lax.ppermute(own, 'dp', down))  15.4 us
    ppermute x6, waiting for transfers between devices, step(): lax.ppermute(a, 'dp', up)  12.9 us
    ppermute x6, starting transfers between devices, step(): lax.ppermute(a, 'dp', up)  11.8 us
    all_to_all x1, starting transfers between devices, exchange(): lax.all_to_all(parts, 'expert', split_axis=0, concat_axis=0, tiled=True)  10.2 us
    all_to_all x1, waiting for transfers between devices, exchange(): lax.all_to_all(parts, 'expert', split_axis=0, concat_axis=0, tiled=True)  9.67 us
  transfers between devices with their start and end apart: 19, of which 6 were waited for; matrix products, arithmetic and copies ran while one was open for 1% of the time, Pallas kernels for 9%

profile of v4, /device:TPU:8, one launch (start us, length us, event | category | flops | bytes accessed | tf_op | source)
XLA Modules:
  0.0 164.9 jit_solution(365525789659330089)
XLA Ops:
  0.8 1.7 %collective-permute-start = (bf16[16,1536]{1,0:T(8,128)(2,1)S(1)}, bf16[16,1536]{1,0:T(8,128)(2,1)S(1)}, u32[]{:S(2)}, u32[]{:S(2)}) collective-permute-start(bf16[16,1536]{1,0:T(8,128)(2,1)S(1)} %get-tuple-element.32), channel_id=1, source_target_pairs={{0,1},{1,2},{2,3},{3,4},{4,5},{5,6},{6,7},{7,8},{8,9},{9,10},{10,1... | collective-permute-start | bytes 147464 | tf_op jit(solution)/shard_map/ppermute | solution.py:229
  2.6 1.4 collective-permute-start.1
  4.1 2.3 %shard_map.74.refs_0_ = bf16[2,192,1536]{2,1,0:T(8,128)(2,1)} custom-call(bf16[1,192,1536]{2,1,0:T(8,128)(2,1)} %first_ref.1, bf16[1,192,1536]{2,1,0:T(8,128)(2,1)} %second_ref.1), custom_call_target="tpu_custom_call" | custom-call | tf_op jit(solution)/shard_map/pallas_call | solution.py:233
  6.4 6.8 %collective-permute-start.3 = (bf16[2,192,1536]{2,1,0:T(8,128)(2,1)}, bf16[2,192,1536]{2,1,0:T(8,128)(2,1)S(1)}, u32[]{:S(2)}, u32[]{:S(2)}) collective-permute-start(bf16[2,192,1536]{2,1,0:T(8,128)(2,1)} %shard_map.74.refs_0_), channel_id=1, source_target_pairs={{0,2},{1,3},{2,4},{3,5},{4,6},{5,7},{6,8},{7,9},{8,10},{9,11},{10,... | collective-permute-start | bytes 3538952 | tf_op jit(solution)/shard_map/ppermute | solution.py:240
  13.2 8.6 %collective-permute-start.4 = (bf16[2,192,1536]{2,1,0:T(8,128)(2,1)}, bf16[2,192,1536]{2,1,0:T(8,128)(2,1)S(1)}, u32[]{:S(2)}, u32[]{:S(2)}) collective-permute-start(bf16[2,192,1536]{2,1,0:T(8,128)(2,1)} %shard_map.74.refs_0_), channel_id=1, source_target_pairs={{0,14},{1,15},{2,0},{3,1},{4,2},{5,3},{6,4},{7,5},{8,6},{9,7},{10,... | collective-permute-start | bytes 3538952 | tf_op jit(solution)/shard_map/ppermute | solution.py:240
  21.9 4.0 %shard_map.73 = (bf16[256,1792]{1,0:T(8,128)(2,1)}, f32[128,1536]{1,0:T(8,128)S(1)}, bf16[128,256]{1,0:T(8,128)(2,1)S(1)}, bf16[128,256]{1,0:T(8,128)(2,1)S(1)},...) custom-call(bf16[128,1536]{1,0:T(8,128)(2,1)S(1)} %bitcast.24, ...), custom_call_target="tpu_custom_call" | custom-call | flops 20000000000 | bytes 2655232 | tf_op jit(solution)/shard_map/pallas_call | solution.py:28
  29.2 10.2 %all-to-all-start = ((bf16[32,8,1792]{2,1,0:T(8,128)(2,1)}), bf16[32,8,1792]{2,1,0:T(8,128)(2,1)}, u32[]{:S(2)}, u32[]{:S(2)}) async-start(bf16[32,8,1792]{2,1,0:T(8,128)(2,1)} %bitcast.6), calls=%async_computation | async-start | bytes 1835008 | tf_op jit(solution)/shard_map/all_to_all | solution.py:255
  39.4 5.5 %collective-permute-done.3.refs_1_ = bf16[2,192,1536]{2,1,0:T(8,128)(2,1)S(1)} collective-permute-done((bf16[2,192,1536]{2,1,0:T(8,128)(2,1)}, bf16[2,192,1536]{2,1,0:T(8,128)(2,1)S(1)}, u32[]{:S(2)}, u32[]{:S(2)}) %collective-permute-start.3) | collective-permute-done | bytes 1179680 | tf_op jit(solution)/shard_map/ppermute | solution.py:240
  46.1 1.9 %collective-permute-start.6 = (bf16[192,1536]{1,0:T(8,128)(2,1)}, bf16[192,1536]{1,0:T(8,128)(2,1)}, u32[]{:S(2)}, u32[]{:S(2)}) collective-permute-start(bf16[192,1536]{1,0:T(8,128)(2,1)} %get-tuple-element.29), channel_id=1, source_target_pairs={{0,2},{1,3},{2,4},{3,5},{4,6},{5,7},{6,8},{7,9},{8,10},{9,11},{10,... | collective-permute-start | bytes 1769480 | tf_op jit(solution)/shard_map/ppermute | solution.py:243
  49.1 5.3 %collective-permute-start.8 = (bf16[192,1536]{1,0:T(8,128)(2,1)}, bf16[192,1536]{1,0:T(8,128)(2,1)}, u32[]{:S(2)}, u32[]{:S(2)}) collective-permute-start(bf16[192,1536]{1,0:T(8,128)(2,1)} %get-tuple-element.27), channel_id=1, source_target_pairs={{0,14},{1,15},{2,0},{3,1},{4,2},{5,3},{6,4},{7,5},{8,6},{9,7},{10,... | collective-permute-start | bytes 1769480 | tf_op jit(solution)/shard_map/ppermute | solution.py:243
  54.3 9.7 %all-to-all-done = bf16[32,8,1792]{2,1,0:T(8,128)(2,1)} async-done(((bf16[32,8,1792]{2,1,0:T(8,128)(2,1)}), bf16[32,8,1792]{2,1,0:T(8,128)(2,1)}, u32[]{:S(2)}, u32[]{:S(2)}) %all-to-all-start) | async-done | bytes 917536 | tf_op jit(solution)/shard_map/all_to_all | solution.py:255
  64.0 1.9 %collective-permute-start.2 = (bf16[256,1792]{1,0:T(8,128)(2,1)}, bf16[256,1792]{1,0:T(8,128)(2,1)S(1)}, u32[]{:S(2)}, u32[]{:S(2)}) collective-permute-start(bf16[256,1792]{1,0:T(8,128)(2,1)} %bitcast.7.mine_ref), channel_id=1, source_target_pairs={{0,1},{1,0},{2,3},{3,2},{4,5},{5,4},{6,7},{7,6},{8,9},{9,8},{10,11... | collective-permute-start | bytes 2752520 | tf_op jit(solution)/shard_map/ppermute | solution.py:259
  65.9 3.7 %collective-permute-start.7 = (bf16[192,1536]{1,0:T(8,128)(2,1)}, bf16[192,1536]{1,0:T(8,128)(2,1)S(1)}, u32[]{:S(2)}, u32[]{:S(2)}) collective-permute-start(bf16[192,1536]{1,0:T(8,128)(2,1)} %get-tuple-element.28), channel_id=1, source_target_pairs={{0,14},{1,15},{2,0},{3,1},{4,2},{5,3},{6,4},{7,5},{8,6},{9,7},{10,... | collective-permute-start | bytes 1769480 | tf_op jit(solution)/shard_map/ppermute | solution.py:243
  69.6 2.2 %collective-permute-start.5 = (bf16[192,1536]{1,0:T(8,128)(2,1)}, bf16[192,1536]{1,0:T(8,128)(2,1)S(1)}, u32[]{:S(2)}, u32[]{:S(2)}) collective-permute-start(bf16[192,1536]{1,0:T(8,128)(2,1)} %get-tuple-element.30), channel_id=1, source_target_pairs={{0,2},{1,3},{2,4},{3,5},{4,6},{5,7},{6,8},{7,9},{8,10},{9,11},{10,... | collective-permute-start | bytes 1769480 | tf_op jit(solution)/shard_map/ppermute | solution.py:243
  71.8 1.9 %collective-permute-start.11 = (bf16[192,1536]{1,0:T(8,128)(2,1)}, bf16[192,1536]{1,0:T(8,128)(2,1)S(1)}, u32[]{:S(2)}, u32[]{:S(2)}) collective-permute-start(bf16[192,1536]{1,0:T(8,128)(2,1)} %collective-permute-done.6.refs_4_), channel_id=1, source_target_pairs={{0,2},{1,3},{2,4},{3,5},{4,6},{5,7},{6,8},{7,9},{8,10},{9,11},{10,... | collective-permute-start | bytes 1769480 | tf_op jit(solution)/shard_map/ppermute | solution.py:243
  73.7 5.1 %collective-permute-start.12 = (bf16[192,1536]{1,0:T(8,128)(2,1)}, bf16[192,1536]{1,0:T(8,128)(2,1)S(1)}, u32[]{:S(2)}, u32[]{:S(2)}) collective-permute-start(bf16[192,1536]{1,0:T(8,128)(2,1)} %collective-permute-done.8.refs_6_), channel_id=1, source_target_pairs={{0,14},{1,15},{2,0},{3,1},{4,2},{5,3},{6,4},{7,5},{8,6},{9,7},{10,... | collective-permute-start | bytes 1769480 | tf_op jit(solution)/shard_map/ppermute | solution.py:243
  78.9 5.3 %collective-permute-done.7.refs_5_ = bf16[192,1536]{1,0:T(8,128)(2,1)S(1)} collective-permute-done((bf16[192,1536]{1,0:T(8,128)(2,1)}, bf16[192,1536]{1,0:T(8,128)(2,1)S(1)}, u32[]{:S(2)}, u32[]{:S(2)}) %collective-permute-start.7) | collective-permute-done | bytes 589856 | tf_op jit(solution)/shard_map/ppermute | solution.py:243
  84.2 4.9 %collective-permute-start.10 = (bf16[192,1536]{1,0:T(8,128)(2,1)S(1)}, bf16[192,1536]{1,0:T(8,128)(2,1)S(1)}, u32[]{:S(2)}, u32[]{:S(2)}) collective-permute-start(bf16[192,1536]{1,0:T(8,128)(2,1)S(1)} %collective-permute-done.7.refs_5_), channel_id=1, source_target_pairs={{0,14},{1,15},{2,0},{3,1},{4,2},{5,3},{6,4},{7,5},{8,6},{9,7},{10,... | collective-permute-start | bytes 1769480 | tf_op jit(solution)/shard_map/ppermute | solution.py:243
  89.1 1.9 %collective-permute-start.9 = (bf16[192,1536]{1,0:T(8,128)(2,1)S(1)}, bf16[192,1536]{1,0:T(8,128)(2,1)S(1)}, u32[]{:S(2)}, u32[]{:S(2)}) collective-permute-start(bf16[192,1536]{1,0:T(8,128)(2,1)S(1)} %collective-permute-done.5.refs_3_), channel_id=1, source_target_pairs={{0,2},{1,3},{2,4},{3,5},{4,6},{5,7},{6,8},{7,9},{8,10},{9,11},{10,... | collective-permute-start | bytes 1769480 | tf_op jit(solution)/shard_map/ppermute | solution.py:243
  91.0 10.7 %collective-permute-done.11.refs_1_ = bf16[192,1536]{1,0:T(8,128)(2,1)S(1)} collective-permute-done((bf16[192,1536]{1,0:T(8,128)(2,1)}, bf16[192,1536]{1,0:T(8,128)(2,1)S(1)}, u32[]{:S(2)}, u32[]{:S(2)}) %collective-permute-start.11) | collective-permute-done | bytes 589856 | tf_op jit(solution)/shard_map/ppermute | solution.py:243
  101.7 1.9 %collective-permute-start.14 = (bf16[96,1536]{1,0:T(8,128)(2,1)S(1)}, bf16[96,1536]{1,0:T(8,128)(2,1)S(1)}, u32[]{:S(2)}, u32[]{:S(2)}) collective-permute-start(bf16[96,1536]{1,0:T(8,128)(2,1)S(1)} %slice.52), channel_id=1, source_target_pairs={{0,2},{1,3},{2,4},{3,5},{4,6},{5,7},{6,8},{7,9},{8,10},{9,11},{10,... | collective-permute-start | bytes 884744 | tf_op jit(solution)/shard_map/ppermute | solution.py:243
  103.7 5.1 %collective-permute-start.16 = (bf16[96,1536]{1,0:T(8,128)(2,1)S(1)}, bf16[96,1536]{1,0:T(8,128)(2,1)S(1)}, u32[]{:S(2)}, u32[]{:S(2)}) collective-permute-start(bf16[96,1536]{1,0:T(8,128)(2,1)S(1)} %slice.53), channel_id=1, source_target_pairs={{0,14},{1,15},{2,0},{3,1},{4,2},{5,3},{6,4},{7,5},{8,6},{9,7},{10,... | collective-permute-start | bytes 884744 | tf_op jit(solution)/shard_map/ppermute | solution.py:243
  108.9 5.8 %shard_map.75 = (bf16[576,1536]{1,0:T(8,128)(2,1)S(1)}, f32[576,1536]{1,0:T(8,128)S(1)}) custom-call(bf16[256,1792]{1,0:T(8,128)(2,1)} %bitcast.7.mine_ref, bf16[256,1792]{1,0:T(8,128)(2,1)S(1)} %collective-permute-done.2.other_ref, bf16[2,192,1536]{2,1,0:T(8,128)(2,1)S(1)} %copy-done, bf16[2,192,1536]{2,1,0:T(8,128)(2,1)S(1)} %collective-permute-done.3.refs_1_, ...), custom_call_target="tpu_custom_call" | custom-call | flops 3397386240 | bytes 13041664 | tf_op jit(solution)/shard_map/pallas_call | solution.py:28
  114.8 1.9 %collective-permute-start.13 = (bf16[96,1536]{1,0:T(8,128)(2,1)S(1)}, bf16[96,1536]{1,0:T(8,128)(2,1)S(1)}, u32[]{:S(2)}, u32[]{:S(2)}) collective-permute-start(bf16[96,1536]{1,0:T(8,128)(2,1)S(1)} %slice.44), channel_id=1, source_target_pairs={{0,2},{1,3},{2,4},{3,5},{4,6},{5,7},{6,8},{7,9},{8,10},{9,11},{10,... | collective-permute-start | bytes 884744 | tf_op jit(solution)/shard_map/ppermute | solution.py:243
  116.7 5.1 %collective-permute-start.15 = (bf16[96,1536]{1,0:T(8,128)(2,1)S(1)}, bf16[96,1536]{1,0:T(8,128)(2,1)S(1)}, u32[]{:S(2)}, u32[]{:S(2)}) collective-permute-start(bf16[96,1536]{1,0:T(8,128)(2,1)S(1)} %slice.46), channel_id=1, source_target_pairs={{0,14},{1,15},{2,0},{3,1},{4,2},{5,3},{6,4},{7,5},{8,6},{9,7},{10,... | collective-permute-start | bytes 884744 | tf_op jit(solution)/shard_map/ppermute | solution.py:243
  121.9 2.3 %shard_map.76.old_ref = f32[576,1536]{1,0:T(8,128)S(1)} custom-call(bf16[576,1536]{1,0:T(8,128)(2,1)S(1)} %get-tuple-element.17.rows_ref, f32[576,1536]{1,0:T(8,128)S(1)} %get-tuple-element.19.old_ref, bf16[192,1536]{1,0:T(8,128)(2,1)S(1)} %collective-permute-done.9.refs_0_, ...), custom_call_target="tpu_custom_call", output_to_operand_aliasing={{}: (1, {})} | custom-call | flops 1358954496 | bytes 11206656 | tf_op jit(solution)/shard_map/pallas_call | solution.py:28
  124.1 2.1 %collective-permute-done.13.refs_0_ = bf16[96,1536]{1,0:T(8,128)(2,1)S(1)} collective-permute-done((bf16[96,1536]{1,0:T(8,128)(2,1)S(1)}, bf16[96,1536]{1,0:T(8,128)(2,1)S(1)}, u32[]{:S(2)}, u32[]{:S(2)}) %collective-permute-start.13) | collective-permute-done | bytes 294944 | tf_op jit(solution)/shard_map/ppermute | solution.py:243
  127.4 1.9 %collective-permute-start.17 = (bf16[288,1536]{1,0:T(8,128)(2,1)S(1)}, bf16[288,1536]{1,0:T(8,128)(2,1)S(1)}, u32[]{:S(2)}, u32[]{:S(2)}) collective-permute-start(bf16[288,1536]{1,0:T(8,128)(2,1)S(1)} %shard_map.78), channel_id=1, source_target_pairs={{0,1},{1,0},{2,3},{3,2},{4,5},{5,4},{6,7},{7,6},{8,9},{9,8},{10,11... | collective-permute-start | bytes 2654216 | tf_op jit(solution)/shard_map/ppermute | solution.py:280
  129.4 1.1 shard_map.77.mine_ref
  130.5 1.2 collective-permute-done.17.other_ref
  132.4 31.1 %all_to_all.10 = bf16[32,8,1792]{2,1,0:T(8,128)(2,1)S(1)} all-to-all(bf16[32,8,1792]{2,1,0:T(8,128)(2,1)S(1)} %bitcast.22), channel_id=1, replica_groups=mesh['expert'=32,'dp'=16] {'expert'}, dimensions={0} | all-to-all | bytes 1835008 | tf_op jit(solution)/shard_map/all_to_all | solution.py:255
  163.6 1.3 shard_map.80
  (55 shorter events, 8.4 us)
Async XLA Ops:
  0.8 21.0 %collective-permute-start = (bf16[16,1536]{1,0:T(8,128)(2,1)S(1)}, bf16[16,1536]{1,0:T(8,128)(2,1)S(1)}, u32[]{:S(2)}, u32[]{:S(2)}) collective-permute-start(bf16[16,1536]{1,0:T(8,128)(2,1)S(1)} %get-tuple-element.32), channel_id=1, source_target_pairs={{0,1},{1,2},{2,3},{3,4},{4,5},{5,6},{6,7},{7,8},{8,9},{9,10},{10,1... | collective-permute-start | bytes 147464 | tf_op jit(solution)/shard_map/ppermute | solution.py:229
  2.6 19.2 %copy-start.15 = (bf16[1536]{0:T(1024)(128)(2,1)S(1)}, bf16[1536]{0:T(1024)(128)(2,1)}, u32[]{:S(2)}) copy-start(bf16[1536]{0:T(1024)(128)(2,1)} %param.9) | copy-start | bytes 9220
  2.6 19.3 %copy-start.11 = (bf16[1,128,1536]{2,1,0:T(8,128)(2,1)S(1)}, bf16[1,128,1536]{2,1,0:T(8,128)(2,1)}, u32[]{:S(2)}) copy-start(bf16[1,128,1536]{2,1,0:T(8,128)(2,1)} %param.7) | copy-start | bytes 1179652
  2.6 19.2 %copy-start.12 = (bf16[31,1536]{1,0:T(8,128)(2,1)S(1)}, bf16[31,1536]{1,0:T(8,128)(2,1)}, u32[]{:S(2)}) copy-start(bf16[31,1536]{1,0:T(8,128)(2,1)} %kernel_ref.1) | copy-start | bytes 285700
  2.6 19.2 %copy-start.13 = (bf16[1536,32]{0,1:T(8,128)(2,1)S(1)}, bf16[1536,32]{0,1:T(8,128)(2,1)}, u32[]{:S(2)}) copy-start(bf16[1536,32]{0,1:T(8,128)(2,1)} %param.10) | copy-start | bytes 294916
  2.6 19.2 %copy-start.14 = (s32[1,128,2]{1,2,0:T(2,128)S(1)}, s32[1,128,2]{1,2,0:T(2,128)}, u32[]{:S(2)}) copy-start(s32[1,128,2]{1,2,0:T(2,128)} %param.13) | copy-start | bytes 3076
  2.6 19.2 %collective-permute-start.1 = (bf16[16,1536]{1,0:T(8,128)(2,1)S(1)}, bf16[16,1536]{1,0:T(8,128)(2,1)S(1)}, u32[]{:S(2)}, u32[]{:S(2)}) collective-permute-start(bf16[16,1536]{1,0:T(8,128)(2,1)S(1)} %get-tuple-element.31), channel_id=1, source_target_pairs={{1,0},{2,1},{3,2},{4,3},{5,4},{6,5},{7,6},{8,7},{9,8},{10,9},{11,1... | collective-permute-start | bytes 147464 | tf_op jit(solution)/shard_map/ppermute | solution.py:230
  6.4 38.6 %collective-permute-start.3 = (bf16[2,192,1536]{2,1,0:T(8,128)(2,1)}, bf16[2,192,1536]{2,1,0:T(8,128)(2,1)S(1)}, u32[]{:S(2)}, u32[]{:S(2)}) collective-permute-start(bf16[2,192,1536]{2,1,0:T(8,128)(2,1)} %shard_map.74.refs_0_), channel_id=1, source_target_pairs={{0,2},{1,3},{2,4},{3,5},{4,6},{5,7},{6,8},{7,9},{8,10},{9,11},{10,... | collective-permute-start | bytes 3538952 | tf_op jit(solution)/shard_map/ppermute | solution.py:240
  13.2 34.8 %collective-permute-start.4 = (bf16[2,192,1536]{2,1,0:T(8,128)(2,1)}, bf16[2,192,1536]{2,1,0:T(8,128)(2,1)S(1)}, u32[]{:S(2)}, u32[]{:S(2)}) collective-permute-start(bf16[2,192,1536]{2,1,0:T(8,128)(2,1)} %shard_map.74.refs_0_), channel_id=1, source_target_pairs={{0,14},{1,15},{2,0},{3,1},{4,2},{5,3},{6,4},{7,5},{8,6},{9,7},{10,... | collective-permute-start | bytes 3538952 | tf_op jit(solution)/shard_map/ppermute | solution.py:240
  25.8 0.9 copy-start.1
  28.0 0.6 copy-start.7
  29.2 34.8 %all-to-all-start = ((bf16[32,8,1792]{2,1,0:T(8,128)(2,1)}), bf16[32,8,1792]{2,1,0:T(8,128)(2,1)}, u32[]{:S(2)}, u32[]{:S(2)}) async-start(bf16[32,8,1792]{2,1,0:T(8,128)(2,1)} %bitcast.6), calls=%async_computation | async-start | bytes 1835008 | tf_op jit(solution)/shard_map/all_to_all | solution.py:255
  46.1 25.7 %collective-permute-start.6 = (bf16[192,1536]{1,0:T(8,128)(2,1)}, bf16[192,1536]{1,0:T(8,128)(2,1)}, u32[]{:S(2)}, u32[]{:S(2)}) collective-permute-start(bf16[192,1536]{1,0:T(8,128)(2,1)} %get-tuple-element.29), channel_id=1, source_target_pairs={{0,2},{1,3},{2,4},{3,5},{4,6},{5,7},{6,8},{7,9},{8,10},{9,11},{10,... | collective-permute-start | bytes 1769480 | tf_op jit(solution)/shard_map/ppermute | solution.py:243
  49.1 59.8 %copy-start = (bf16[2,192,1536]{2,1,0:T(8,128)(2,1)S(1)}, bf16[2,192,1536]{2,1,0:T(8,128)(2,1)}, u32[]{:S(2)}) copy-start(bf16[2,192,1536]{2,1,0:T(8,128)(2,1)} %shard_map.74.refs_0_) | copy-start | bytes 3538948
  49.1 24.6 %collective-permute-start.8 = (bf16[192,1536]{1,0:T(8,128)(2,1)}, bf16[192,1536]{1,0:T(8,128)(2,1)}, u32[]{:S(2)}, u32[]{:S(2)}) collective-permute-start(bf16[192,1536]{1,0:T(8,128)(2,1)} %get-tuple-element.27), channel_id=1, source_target_pairs={{0,14},{1,15},{2,0},{3,1},{4,2},{5,3},{6,4},{7,5},{8,6},{9,7},{10,... | collective-permute-start | bytes 1769480 | tf_op jit(solution)/shard_map/ppermute | solution.py:243
  64.0 44.8 %collective-permute-start.2 = (bf16[256,1792]{1,0:T(8,128)(2,1)}, bf16[256,1792]{1,0:T(8,128)(2,1)S(1)}, u32[]{:S(2)}, u32[]{:S(2)}) collective-permute-start(bf16[256,1792]{1,0:T(8,128)(2,1)} %bitcast.7.mine_ref), channel_id=1, source_target_pairs={{0,1},{1,0},{2,3},{3,2},{4,5},{5,4},{6,7},{7,6},{8,9},{9,8},{10,11... | collective-permute-start | bytes 2752520 | tf_op jit(solution)/shard_map/ppermute | solution.py:259
  65.9 18.2 %collective-permute-start.7 = (bf16[192,1536]{1,0:T(8,128)(2,1)}, bf16[192,1536]{1,0:T(8,128)(2,1)S(1)}, u32[]{:S(2)}, u32[]{:S(2)}) collective-permute-start(bf16[192,1536]{1,0:T(8,128)(2,1)} %get-tuple-element.28), channel_id=1, source_target_pairs={{0,14},{1,15},{2,0},{3,1},{4,2},{5,3},{6,4},{7,5},{8,6},{9,7},{10,... | collective-permute-start | bytes 1769480 | tf_op jit(solution)/shard_map/ppermute | solution.py:243
  69.6 19.5 %collective-permute-start.5 = (bf16[192,1536]{1,0:T(8,128)(2,1)}, bf16[192,1536]{1,0:T(8,128)(2,1)S(1)}, u32[]{:S(2)}, u32[]{:S(2)}) collective-permute-start(bf16[192,1536]{1,0:T(8,128)(2,1)} %get-tuple-element.30), channel_id=1, source_target_pairs={{0,2},{1,3},{2,4},{3,5},{4,6},{5,7},{6,8},{7,9},{8,10},{9,11},{10,... | collective-permute-start | bytes 1769480 | tf_op jit(solution)/shard_map/ppermute | solution.py:243
  71.8 29.9 %collective-permute-start.11 = (bf16[192,1536]{1,0:T(8,128)(2,1)}, bf16[192,1536]{1,0:T(8,128)(2,1)S(1)}, u32[]{:S(2)}, u32[]{:S(2)}) collective-permute-start(bf16[192,1536]{1,0:T(8,128)(2,1)} %collective-permute-done.6.refs_4_), channel_id=1, source_target_pairs={{0,2},{1,3},{2,4},{3,5},{4,6},{5,7},{6,8},{7,9},{8,10},{9,11},{10,... | collective-permute-start | bytes 1769480 | tf_op jit(solution)/shard_map/ppermute | solution.py:243
  73.7 29.9 %collective-permute-start.12 = (bf16[192,1536]{1,0:T(8,128)(2,1)}, bf16[192,1536]{1,0:T(8,128)(2,1)S(1)}, u32[]{:S(2)}, u32[]{:S(2)}) collective-permute-start(bf16[192,1536]{1,0:T(8,128)(2,1)} %collective-permute-done.8.refs_6_), channel_id=1, source_target_pairs={{0,14},{1,15},{2,0},{3,1},{4,2},{5,3},{6,4},{7,5},{8,6},{9,7},{10,... | collective-permute-start | bytes 1769480 | tf_op jit(solution)/shard_map/ppermute | solution.py:243
  84.2 30.6 %collective-permute-start.10 = (bf16[192,1536]{1,0:T(8,128)(2,1)S(1)}, bf16[192,1536]{1,0:T(8,128)(2,1)S(1)}, u32[]{:S(2)}, u32[]{:S(2)}) collective-permute-start(bf16[192,1536]{1,0:T(8,128)(2,1)S(1)} %collective-permute-done.7.refs_5_), channel_id=1, source_target_pairs={{0,14},{1,15},{2,0},{3,1},{4,2},{5,3},{6,4},{7,5},{8,6},{9,7},{10,... | collective-permute-start | bytes 1769480 | tf_op jit(solution)/shard_map/ppermute | solution.py:243
  89.1 25.6 %collective-permute-start.9 = (bf16[192,1536]{1,0:T(8,128)(2,1)S(1)}, bf16[192,1536]{1,0:T(8,128)(2,1)S(1)}, u32[]{:S(2)}, u32[]{:S(2)}) collective-permute-start(bf16[192,1536]{1,0:T(8,128)(2,1)S(1)} %collective-permute-done.5.refs_3_), channel_id=1, source_target_pairs={{0,2},{1,3},{2,4},{3,5},{4,6},{5,7},{6,8},{7,9},{8,10},{9,11},{10,... | collective-permute-start | bytes 1769480 | tf_op jit(solution)/shard_map/ppermute | solution.py:243
  101.7 22.4 %collective-permute-start.14 = (bf16[96,1536]{1,0:T(8,128)(2,1)S(1)}, bf16[96,1536]{1,0:T(8,128)(2,1)S(1)}, u32[]{:S(2)}, u32[]{:S(2)}) collective-permute-start(bf16[96,1536]{1,0:T(8,128)(2,1)S(1)} %slice.52), channel_id=1, source_target_pairs={{0,2},{1,3},{2,4},{3,5},{4,6},{5,7},{6,8},{7,9},{8,10},{9,11},{10,... | collective-permute-start | bytes 884744 | tf_op jit(solution)/shard_map/ppermute | solution.py:243
  103.7 20.4 %collective-permute-start.16 = (bf16[96,1536]{1,0:T(8,128)(2,1)S(1)}, bf16[96,1536]{1,0:T(8,128)(2,1)S(1)}, u32[]{:S(2)}, u32[]{:S(2)}) collective-permute-start(bf16[96,1536]{1,0:T(8,128)(2,1)S(1)} %slice.53), channel_id=1, source_target_pairs={{0,14},{1,15},{2,0},{3,1},{4,2},{5,3},{6,4},{7,5},{8,6},{9,7},{10,... | collective-permute-start | bytes 884744 | tf_op jit(solution)/shard_map/ppermute | solution.py:243
  114.8 11.5 %collective-permute-start.13 = (bf16[96,1536]{1,0:T(8,128)(2,1)S(1)}, bf16[96,1536]{1,0:T(8,128)(2,1)S(1)}, u32[]{:S(2)}, u32[]{:S(2)}) collective-permute-start(bf16[96,1536]{1,0:T(8,128)(2,1)S(1)} %slice.44), channel_id=1, source_target_pairs={{0,2},{1,3},{2,4},{3,5},{4,6},{5,7},{6,8},{7,9},{8,10},{9,11},{10,... | collective-permute-start | bytes 884744 | tf_op jit(solution)/shard_map/ppermute | solution.py:243
  116.7 9.6 %collective-permute-start.15 = (bf16[96,1536]{1,0:T(8,128)(2,1)S(1)}, bf16[96,1536]{1,0:T(8,128)(2,1)S(1)}, u32[]{:S(2)}, u32[]{:S(2)}) collective-permute-start(bf16[96,1536]{1,0:T(8,128)(2,1)S(1)} %slice.46), channel_id=1, source_target_pairs={{0,14},{1,15},{2,0},{3,1},{4,2},{5,3},{6,4},{7,5},{8,6},{9,7},{10,... | collective-permute-start | bytes 884744 | tf_op jit(solution)/shard_map/ppermute | solution.py:243
  127.4 4.3 %collective-permute-start.17 = (bf16[288,1536]{1,0:T(8,128)(2,1)S(1)}, bf16[288,1536]{1,0:T(8,128)(2,1)S(1)}, u32[]{:S(2)}, u32[]{:S(2)}) collective-permute-start(bf16[288,1536]{1,0:T(8,128)(2,1)S(1)} %shard_map.78), channel_id=1, source_target_pairs={{0,1},{1,0},{2,3},{3,2},{4,5},{5,4},{6,7},{7,6},{8,9},{9,8},{10,11... | collective-permute-start | bytes 2654216 | tf_op jit(solution)/shard_map/ppermute | solution.py:280
  132.4 31.2 %copy-start.2 = (f32[128,1536]{1,0:T(8,128)S(1)}, f32[128,1536]{1,0:T(8,128)}, u32[]{:S(2)}) copy-start(f32[128,1536]{1,0:T(8,128)} %copy-done.1) | copy-start | bytes 2359300
  132.4 31.2 %copy-start.4 = (bf16[128,256]{1,0:T(8,128)(2,1)S(1)}, bf16[128,256]{1,0:T(8,128)(2,1)}, u32[]{:S(2)}) copy-start(bf16[128,256]{1,0:T(8,128)(2,1)} %copy-done.3) | copy-start | bytes 196612
  132.4 31.2 %copy-start.6 = (bf16[128,256]{1,0:T(8,128)(2,1)S(1)}, bf16[128,256]{1,0:T(8,128)(2,1)}, u32[]{:S(2)}) copy-start(bf16[128,256]{1,0:T(8,128)(2,1)} %copy-done.5) | copy-start | bytes 196612
  132.4 31.2 %copy-start.8 = (bf16[128,256]{1,0:T(8,128)(2,1)S(1)}, bf16[128,256]{1,0:T(8,128)(2,1)}, u32[]{:S(2)}) copy-start(bf16[128,256]{1,0:T(8,128)(2,1)} %copy-done.7) | copy-start | bytes 196612
  132.4 31.2 %copy-start.10 = (bf16[128,256]{1,0:T(8,128)(2,1)S(1)}, bf16[128,256]{1,0:T(8,128)(2,1)}, u32[]{:S(2)}) copy-start(bf16[128,256]{1,0:T(8,128)(2,1)} %copy-done.9) | copy-start | bytes 196612
  (3 other events, 1.9 us)
